TPU v7x, 1024 devices: a whole 4x4x32 slice. The times are simulated.
1024 devices in a mesh: curve: 128 (over x, z), group: 8 (over y, core).
Axes of the slice: x: 4, y: 4, z: 32, core: 2. Of those that a mesh axis runs over, the one named last changes fastest.
Arguments:
- right_side: float32 [64, 262144], P(None, ('curve', 'group')), may hold values from -6 to 6
- start_field: float32 [64, 262144], P(None, ('curve', 'group')), may hold values from -3 to 3
- block_level: int32 [262144], P(('curve', 'group')), may hold values from 0 to 3
- neighbors: int32 [8, 262144], P(None, ('curve', 'group')), may hold values from -64 to 64, as said below
- neighbor_kinds: int32 [8, 262144], P(None, ('curve', 'group')), may hold values from 0 to 29
- owners_zero: int32 [2, 262144], P(None, ('curve', 'group')), may hold values from 0 to 63, as said below
- owners_one: int32 [2, 65536], P(None, 'curve'), may hold values from 0 to 127, as said below
- owners_two: int32 [2, 16384], P(None, 'curve'), may hold values from 0 to 31, as said below
- owners_three: int32 [2, 4096], replicated, may hold values from 0 to 7, as said below
- coarse_neighbors: int32 [8, 1024], replicated, may hold values from -1 to 1023, as said below
- coarse_kinds: int32 [8, 1024], replicated, may hold values from 0 to 29
- coarse_level: int32 [1024], replicated, may hold values from 0 to 3
- stiffness: float32 [64, 64], replicated
- smoother: float32 [64, 64], replicated
- couplings: float32 [30, 64, 64], replicated, may hold values from -0.18 to 0.18
- restriction: float32 [8, 64, 64], replicated, may hold values from -0.375 to 0.375
Outputs:
- smoothed: float32 [64, 262144], P(None, ('curve', 'group'))
Inputs may be any that keep to these rules, and one draw needn't show every extreme that they name: `neighbors`: 0 where a slot couples to nothing, else the nonzero offset to another fine block inside the grid; in slot 0 the first block of each device's range has offset exactly -64 and the last exactly 64 wherever that neighbour exists. `owners_zero`: row 0: within each device's 256 blocks, slots of 64 level-one blocks that never fall, every slot used by 1 to 8 blocks and by 8 in some; row 1: octant. `owners_one`: row 0: within each curve index's level-one blocks, slots of 128 level-two blocks that never fall, every slot used by 1 to 8 blocks and by 8 in some; row 1: octant. `owners_two`: row 0: within each curve index's 128 blocks, slots of 32 level-three blocks that never fall, every slot used by 1 to 8 blocks and by 8 in some; row 1: octant. `owners_three`: row 0: within each curve index's 32 blocks, slots of 8 level-four blocks that never fall, every slot used by 1 to 8 blocks and by 8 in some; row 1: octant. `coarse_neighbors`: -1 where a slot couples to nothing, else another level-four block.
All inputs are finite; a program needn't handle non-finite values.
Results may differ from a plain program's by a relative error of at most 0.0003.
Values sent between devices are 32-bit elements; how exact they have to be, the bound alone decides.
No kernel may reach another device: no remote copies, remote signals or barrier semaphores. Data moves between devices by JAX's collectives and lax.ppermute only.
A program may use at most 64 MiB of HBM per device.

v0:
```python
import jax
import jax.numpy as jnp
from jax import lax
from jax.experimental import pallas as pl
from jax.experimental.pallas import tpu as pltpu
from jax.sharding import PartitionSpec as P

HALO = 64
DAMPING = 0.7
F32 = jnp.float32
BF16 = jnp.bfloat16
VMEM_LIMIT = 40 * 1024 * 1024


def halves(x):
    high = x.astype(BF16)
    return high, (x - high.astype(F32)).astype(BF16)


def nn(a, b):
    return lax.dot_general(a, b, (((1,), (0,)), ((), ())), preferred_element_type=F32)


def nt(a, b):
    return lax.dot_general(a, b, (((1,), (1,)), ((), ())), preferred_element_type=F32)


def corners(product):
    half = product.shape[1] // 2
    top, low = product[:64], product[64:]
    return top[:, :half] + (top[:, half:] + low[:, :half]) + low[:, half:]


def wide_dot(matrix_pair, x):
    high, low = halves(x)
    return corners(nn(matrix_pair, jnp.concatenate([high, low], axis=1)))


def stacked(x):
    return jnp.concatenate(halves(x), axis=0)


def folded(x):
    half = x.shape[0] // 2
    return x[:half] + x[half:]


def onehot_rows(row_count, columns):
    rows = lax.broadcasted_iota(jnp.int32, (row_count, columns.shape[1]), 0)
    return jnp.where(rows == columns, 1.0, 0.0).astype(BF16)


def left_by(x, lanes):
    size = x.shape[1]
    return pltpu.roll(x, (size - lanes) % size, axis=1)


def couple(slot_values, kinds, own, coupling_pair):
    total = None
    for part in range(8):
        pieces = []
        for kind in range(4 * part, 4 * part + 4):
            if kind < 30:
                chosen = None
                for slot in range(8):
                    term = jnp.where(kinds[slot : slot + 1] == kind, slot_values[slot], 0.0)
                    chosen = term if chosen is None else chosen + term
            elif kind == 30:
                chosen = own
            else:
                chosen = jnp.zeros_like(own)
            pieces.append(jnp.concatenate(halves(chosen), axis=1))
        block = jnp.concatenate(pieces, axis=0)
        product = nn(coupling_pair[:, 256 * part : 256 * part + 256], block)
        total = product if total is None else total + product
    return corners(total)


def fine_tile(window, offsets, kinds, coupling_pair, slots):
    lanes = lax.broadcasted_iota(jnp.int32, offsets.shape, 1)
    targets = jnp.where(offsets != 0, lanes + offsets + HALO, -1)
    window_pair = stacked(window)
    for slot in range(0, 8, 2):
        columns = jnp.concatenate([targets[slot : slot + 1], targets[slot + 1 : slot + 2]], axis=1)
        picked = folded(nn(window_pair, onehot_rows(256, columns)))
        slots[slot] = picked[:, :128]
        slots[slot + 1] = picked[:, 128:]
    own = left_by(window, HALO)[:, :128]
    return couple(slots, kinds, own, coupling_pair), own


def by_octant(x, octant):
    return jnp.concatenate([jnp.where(octant == which, x, 0.0) for which in range(8)], axis=0)


def restrict(x, slot, octant, restriction_pair, parents):
    mapped = wide_dot(restriction_pair, by_octant(x, octant))
    return folded(nt(stacked(mapped), onehot_rows(parents, slot)))


def prolong(x, slot, octant, back_pair):
    pulled = folded(nn(stacked(x), onehot_rows(x.shape[1], slot)))
    return wide_dot(back_pair, by_octant(pulled, octant))


def power(levels):
    return jnp.left_shift(jnp.ones_like(levels), levels).astype(F32)


def inverse_power(levels):
    return jnp.where(levels == 0, 1.0, jnp.where(levels == 1, 0.5, jnp.where(levels == 2, 0.25, 0.125)))


def prepare_kernel(
    place,
    couplings,
    stiffness,
    smoother,
    restriction,
    owners_one,
    owners_two,
    owners_three,
    coarse_neighbors,
    coarse_kinds,
    coarse_level,
    coupling_pair,
    smoother_pair,
    restriction_pair,
    back_pair,
    table,
):
    def store(target, first, x):
        high, low = halves(x)
        target[0:64, first : first + x.shape[1]] = high
        target[64:128, first : first + x.shape[1]] = low

    for part in range(15):
        store(
            coupling_pair,
            128 * part,
            jnp.concatenate([couplings[2 * part], couplings[2 * part + 1]], axis=1),
        )
    store(
        coupling_pair,
        1920,
        jnp.concatenate([stiffness[...], jnp.zeros((64, 64), F32)], axis=1),
    )
    store(smoother_pair, 0, DAMPING * smoother[...])
    for part in range(4):
        first, second = restriction[2 * part], restriction[2 * part + 1]
        store(restriction_pair, 128 * part, jnp.concatenate([first, second], axis=1))
        upright = jnp.concatenate([first, second], axis=0)
        square = jnp.concatenate([upright, jnp.zeros((128, 64), F32)], axis=1)
        store(back_pair, 128 * part, jnp.transpose(square)[0:64])

    member, group = place[0], place[1]
    lanes = lax.broadcasted_iota(jnp.int32, (8, 128), 1)

    def own(ref, rows, block, per, valid):
        share = 128 // per
        first = pl.multiple_of((block // share) * 128, 128)
        held = ref[0:rows, pl.ds(first, 128)]
        if rows == 1:
            held = jnp.broadcast_to(held, (8, 128))
        shift = lax.rem(128 - per * lax.rem(block, share), 128)
        moved = pltpu.roll(held, shift, axis=1)
        return jnp.where(lanes < per, moved, valid)

    def rows_of(ref, block, per):
        share = 128 // per
        first = pl.multiple_of((block // share) * 128, 128)
        shift = lax.rem(128 - per * lax.rem(block, share), 128)
        made = []
        for row in range(2):
            held = jnp.broadcast_to(ref[row : row + 1, pl.ds(first, 128)], (8, 128))
            moved = held if per == 128 else pltpu.roll(held, shift, axis=1)
            made.append(jnp.where(lanes < per, moved, -1)[0:1])
        return made

    zero = jnp.int32(0)
    for at, (ref, block, per) in enumerate(
        ((owners_one, group, 64), (owners_two, zero, 128), (owners_three, member, 32))
    ):
        slot, octant = rows_of(ref, block, per)
        table[2 * at : 2 * at + 1] = slot
        table[2 * at + 1 : 2 * at + 2] = octant
    table[6:7] = own(coarse_level, 1, member, 8, 0)[0:1]
    table[7:8] = jnp.zeros((1, 128), jnp.int32)
    near = own(coarse_neighbors, 8, member, 8, -1)
    table[8:16] = near
    table[16:24] = jnp.where(near >= 0, own(coarse_kinds, 8, member, 8, -1), -1)


def pack_kernel(right_side, start_field, block_level, neighbors, neighbor_kinds, up, down):
    lane = lax.broadcasted_iota(jnp.int32, (32, 128), 1)
    low, high = start_field[:, 0:128], start_field[:, 128:256]
    up[0:64] = high
    up[64:96] = jnp.where(lane < 64, left_by(low[0:32], 64), low[32:64])
    down[0:64] = low
    down[64:96] = jnp.where(lane < 64, high[0:32], left_by(high[32:64], 64))
    for target, columns in ((up, slice(128, 256)), (down, slice(0, 128))):
        target[96:160] = right_side[:, columns]
        target[160:168] = neighbors[:, columns].astype(F32)
        target[168:176] = neighbor_kinds[:, columns].astype(F32)
        target[176:184] = jnp.broadcast_to(block_level[:, columns], (8, 128)).astype(F32)


def before_kernel(
    left,
    right_side,
    start_field,
    block_level,
    neighbors,
    neighbor_kinds,
    right,
    owners_zero,
    coupling_pair,
    smoother_pair,
    restriction_pair,
    table,
    iterate_out,
    part_out,
    first,
    second,
    third,
    facts_wide,
    facts_narrow,
    remainder,
    slots,
):
    matrix = coupling_pair
    far_left, far_right = left[64:96], right[64:96]
    row = jnp.concatenate(
        [
            jnp.concatenate([left_by(far_left, 64), far_left], axis=0),
            left[0:64],
            start_field[...],
            right[0:64],
            jnp.concatenate([far_right, left_by(far_right, 64)], axis=0),
        ],
        axis=1,
    )
    first[...] = left_by(row, 64)[:, :640]
    numbers = jnp.concatenate(
        [
            neighbors[...],
            neighbor_kinds[...],
            jnp.broadcast_to(block_level[...], (8, 256)),
        ],
        axis=0,
    )
    own = jnp.concatenate([right_side[...], numbers.astype(F32)], axis=0)
    facts = jnp.concatenate([left[96:184], own, right[96:184]], axis=1)
    facts_wide[...] = facts
    facts_narrow[...] = left_by(facts, 64)[:, :384]

    def image(source, facts_of, at):
        start = pl.multiple_of(128 * at, 128)
        window = source[:, pl.ds(start, 256)]
        here = facts_of[:, pl.ds(start, 128)]
        offsets = here[64:72].astype(jnp.int32)
        kinds = here[72:80].astype(jnp.int32)
        levels = here[80:81].astype(jnp.int32)
        applied, held = fine_tile(window, offsets, kinds, matrix[...], slots)
        return start, here[0:64], levels, applied, held

    def sweep(source, facts_of, target):
        def one(at, carry):
            start, rhs, levels, applied, held = image(source, facts_of, at)
            change = wide_dot(smoother_pair[...], rhs * power(levels) - applied)
            target[:, pl.ds(start, 128)] = held + change
            return carry

        return one

    lax.fori_loop(0, 4, sweep(first, facts_wide, second), 0)
    lax.fori_loop(0, 3, sweep(second, facts_narrow, third), 0)

    def last(at, carry):
        start, rhs, levels, applied, held = image(third, facts_wide.at[:, 128:384], at)
        remainder[:, pl.ds(start, 128)] = rhs - inverse_power(levels) * applied
        iterate_out[:, pl.ds(start, 128)] = held
        return carry

    lax.fori_loop(0, 2, last, 0)

    r_pair = restriction_pair[...]
    one = restrict(remainder[...], owners_zero[0:1], owners_zero[1:2], r_pair, 128)
    two = restrict(one, table[0:1], table[1:2], r_pair, 128)
    three = restrict(two, table[2:3], table[3:4], r_pair, 128)
    four = restrict(three, table[4:5], table[5:6], r_pair, 128)
    four = four * power(table[6:7])
    both = jnp.concatenate([four, left_by(four, 4)], axis=0)
    part_out[...] = jnp.transpose(both)[0:4]


def coarse_kernel(
    place,
    gathered,
    table,
    coarse_neighbors,
    coarse_kinds,
    coupling_pair,
    smoother_pair,
    back_pair,
    owners_zero,
    iterate,
    iterate_out,
    low_edge,
    high_edge,
    slots,
):
    member = place[0]
    field_pair = stacked(jnp.transpose(gathered[...]))
    s_pair = smoother_pair[...]
    matrix = coupling_pair[...]

    def gather(blocks):
        known = blocks >= 0
        rows = jnp.where(known, 4 * (blocks >> 3) + (blocks & 3), -1)
        both = folded(nn(field_pair, onehot_rows(512, rows)))
        return jnp.where(((blocks >> 2) & 1) == 0, both[0:64], both[64:128])

    lanes = lax.broadcasted_iota(jnp.int32, (1, 128), 1)
    near = table[8:16]
    near_kinds = table[16:24]
    wanted = jnp.where((lanes >= 64) & (lanes < 72), 8 * member + lanes - 64, -1)
    for slot in range(8):
        moved = pltpu.roll(near, 8 * slot, axis=1) if slot else near
        wanted = jnp.where((lanes >> 3) == slot, moved[slot : slot + 1], wanted)
    shifted = coarse_neighbors[...] + 1
    facts = jnp.concatenate(
        [shifted >> 5, shifted & 31, coarse_kinds[...], jnp.zeros_like(shifted)], axis=0
    ).astype(F32).astype(BF16)
    found = nn(facts, onehot_rows(1024, wanted)).astype(jnp.int32)
    links = 32 * found[0:8] + found[8:16] - 1
    link_kinds = found[16:24]

    for slot in range(0, 8, 2):
        blocks = jnp.concatenate([links[slot : slot + 1], links[slot + 1 : slot + 2]], axis=1)
        swept = wide_dot(s_pair, gather(blocks))
        slots[slot] = swept[:, :128]
        slots[slot + 1] = swept[:, 128:]
    rhs = gather(wanted)
    once = wide_dot(s_pair, rhs)
    twice = once + wide_dot(s_pair, rhs - couple(slots, link_kinds, once, matrix))
    for slot in range(8):
        slots[slot] = left_by(twice, 8 * slot) if slot else twice
    held = left_by(twice, 64)
    applied = couple(slots, near_kinds, held, matrix)
    correction = held + wide_dot(s_pair, left_by(rhs, 64) - applied)

    b_pair = back_pair[...]
    three = prolong(correction, table[4:5], table[5:6], b_pair)
    two = prolong(three, table[2:3], table[3:4], b_pair)
    one = prolong(two, table[0:1], table[1:2], b_pair)
    zero = prolong(one, owners_zero[0:1], owners_zero[1:2], b_pair)
    field = iterate[...] + zero
    iterate_out[...] = field
    low, high = field[:, 0:128], left_by(field[:, 128:256], 64)
    lane = lax.broadcasted_iota(jnp.int32, (32, 128), 1)
    low_edge[...] = jnp.where(lane < 64, low[0:32], left_by(low[32:64], 64))
    high_edge[...] = jnp.where(lane < 64, high[0:32], left_by(high[32:64], 64))


def after_kernel(
    left,
    field,
    right,
    right_side,
    block_level,
    neighbors,
    neighbor_kinds,
    coupling_pair,
    smoother_pair,
    out,
    window_all,
    slots,
):
    def wide(edge):
        return jnp.concatenate([edge[...], left_by(edge[...], 64)], axis=0)

    row = jnp.concatenate([wide(left), field[...], wide(right)], axis=1)
    lanes = lax.broadcasted_iota(jnp.int32, (64, 384), 1)
    body = left_by(row, 64)
    window_all[...] = jnp.where(lanes < 64, row[:, 0:384], body[:, 0:384])

    def one(at, carry):
        start = pl.multiple_of(128 * at, 128)
        columns = pl.ds(start, 128)
        applied, held = fine_tile(
            window_all[:, pl.ds(start, 256)],
            neighbors[:, columns],
            neighbor_kinds[:, columns],
            coupling_pair[...],
            slots,
        )
        rhs = right_side[:, columns] * power(block_level[:, columns])
        out[:, pl.ds(start, 128)] = held + wide_dot(
            smoother_pair[...], rhs - applied
        )
        return carry

    lax.fori_loop(0, 2, one, 0)


def call(kernel, outs, scratch, name, flops, *args, scalars=0):
    specs = [pl.BlockSpec(memory_space=pltpu.SMEM)] * scalars
    specs += [pl.BlockSpec(memory_space=pltpu.VMEM)] * (len(args) - scalars)
    return pl.pallas_call(
        kernel,
        out_shape=[jax.ShapeDtypeStruct(shape, dtype) for shape, dtype in outs],
        in_specs=specs,
        out_specs=[pl.BlockSpec(memory_space=pltpu.VMEM)] * len(outs),
        scratch_shapes=[pltpu.VMEM(shape, dtype) for shape, dtype in scratch],
        compiler_params=pltpu.CompilerParams(vmem_limit_bytes=VMEM_LIMIT),
        cost_estimate=pl.CostEstimate(flops=flops, bytes_accessed=1 << 20, transcendentals=0),
        name=name,
    )(*args)


AXES = ("curve", "group")


def both_ways(up_part, down_part):
    peers = lax.axis_size(AXES)
    up = [(i, i + 1) for i in range(peers - 1)]
    down = [(i + 1, i) for i in range(peers - 1)]
    return lax.ppermute(up_part, AXES, up), lax.ppermute(down_part, AXES, down)


DEPTH = 32
WIDTH = 4


def spread(x, axis, count, groups=None):
    copies = jnp.broadcast_to(x[None], (count,) + x.shape)
    return lax.all_to_all(copies, axis, 0, 0, axis_index_groups=groups)


def share_coarse(part):
    along_z = [[x * DEPTH + z for z in range(DEPTH)] for x in range(WIDTH)]
    along_x = [[x * DEPTH + z for x in range(WIDTH)] for z in range(DEPTH)]
    total = jnp.sum(spread(part, "group", 8), axis=0)
    column = spread(total, "curve", DEPTH, along_z)
    return spread(column, "curve", WIDTH, along_x)


def stage_prepare(place, *args):
    outs = (
        ((128, 2048), BF16),
        ((128, 64), BF16),
        ((128, 512), BF16),
        ((128, 512), BF16),
        ((24, 128), jnp.int32),
    )
    return call(prepare_kernel, outs, (), "prepare", 1 << 20, place, *args, scalars=1)


def stage_before(*args):
    outs = (((64, 256), F32), ((4, 128), F32))
    scratch = (
        ((64, 640), F32),
        ((64, 512), F32),
        ((64, 384), F32),
        ((88, 512), F32),
        ((88, 384), F32),
        ((64, 256), F32),
        ((8, 64, 128), F32),
    )
    return call(before_kernel, outs, scratch, "before", 1 << 31, *args)


def stage_coarse(place, *args):
    outs = (((64, 256), F32), ((32, 128), F32), ((32, 128), F32))
    scratch = (((8, 64, 128), F32),)
    return call(coarse_kernel, outs, scratch, "coarse", 1 << 30, place, *args, scalars=1)


def stage_after(*args):
    scratch = (((64, 384), F32), ((8, 64, 128), F32))
    return call(after_kernel, (((64, 256), F32),), scratch, "after", 1 << 29, *args)


def stage_pack(*args):
    outs = (((184, 128), F32), ((184, 128), F32))
    return call(pack_kernel, outs, (), "pack", 1 << 20, *args)


def shards(
    right_side,
    start_field,
    block_level,
    neighbors,
    neighbor_kinds,
    owners_zero,
    owners_one,
    owners_two,
    owners_three,
    coarse_neighbors,
    coarse_kinds,
    coarse_level,
    stiffness,
    smoother,
    couplings,
    restriction,
):
    place = jnp.stack([lax.axis_index("curve"), lax.axis_index("group")]).astype(jnp.int32)
    fine = (right_side, start_field, block_level[None, :], neighbors, neighbor_kinds)
    left, right = both_ways(*stage_pack(*fine))
    coupling_pair, smoother_pair, restriction_pair, back_pair, table = stage_prepare(
        place,
        couplings,
        stiffness,
        smoother,
        restriction,
        owners_one,
        owners_two,
        owners_three,
        coarse_neighbors,
        coarse_kinds,
        coarse_level[None, :],
    )
    iterate, part = stage_before(
        left, *fine, right, owners_zero, coupling_pair, smoother_pair, restriction_pair, table
    )
    gathered = share_coarse(part)
    gathered = gathered.reshape(-1, gathered.shape[-1])
    field, low_edge, high_edge = stage_coarse(
        place,
        gathered,
        table,
        coarse_neighbors,
        coarse_kinds,
        coupling_pair,
        smoother_pair,
        back_pair,
        owners_zero,
        iterate,
    )
    left_edge, right_edge = both_ways(high_edge, low_edge)
    (out,) = stage_after(
        left_edge,
        field,
        right_edge,
        right_side,
        block_level[None, :],
        neighbors,
        neighbor_kinds,
        coupling_pair,
        smoother_pair,
    )
    return out


def solution(mesh):
    fine = P(None, ("curve", "group"))
    return jax.shard_map(
        shards,
        mesh=mesh,
        in_specs=(
            fine,
            fine,
            P(("curve", "group")),
            fine,
            fine,
            fine,
            P(None, "curve"),
            P(None, "curve"),
            P(),
            P(),
            P(),
            P(),
            P(),
            P(),
            P(),
            P(),
        ),
        out_specs=fine,
        check_vma=False,
    )
```

profile of v0, /device:TPU:2, one launch (start us, length us, event | category | flops | bytes accessed | tf_op | source)
XLA Modules:
  0.0 121.6 jit_solution(14474684909526371416)
XLA Ops:
  0.0 0.0 copy-start.17
  0.0 0.7 copy-done.17
  0.7 0.0 copy-start.2
  0.7 0.8 copy-done.2
  1.5 0.0 copy-start.4
  1.5 0.8 copy-done.4
  2.4 0.0 copy-start.11
  2.4 0.7 copy-done.11
  3.1 0.0 copy-start.13
  3.1 0.7 copy-done.13
  3.8 0.0 copy-start.6
  3.8 0.0 copy-start.7
  3.8 0.0 copy-start.8
  3.8 0.0 copy-start.9
  3.8 0.0 copy-start.10
  3.8 0.1 pack.1
  3.9 1.9 %collective-permute-start = (f32[184,128]{1,0:T(8,128)S(1)}, f32[184,128]{1,0:T(8,128)S(1)}, u32[]{:S(2)}, u32[]{:S(2)}) collective-permute-start(f32[184,128]{1,0:T(8,128)S(1)} %get-tuple-element.17), channel_id=1, source_target_pairs={{0,1},{1,2},{2,3},{3,4},{4,5},{5,6},{6,7},{7,8},{8,9},{9,10},{10,1... | collective-permute-start | bytes 282632 | tf_op jit(solution)/shard_map/ppermute | solution.py:429
  5.8 20.5 %collective-permute-start.1 = (f32[184,128]{1,0:T(8,128)S(1)}, f32[184,128]{1,0:T(8,128)S(1)}, u32[]{:S(2)}, u32[]{:S(2)}) collective-permute-start(f32[184,128]{1,0:T(8,128)S(1)} %get-tuple-element.18), channel_id=1, source_target_pairs={{1,0},{2,1},{3,2},{4,3},{5,4},{6,5},{7,6},{8,7},{9,8},{10,9},{11,1... | collective-permute-start | bytes 282632 | tf_op jit(solution)/shard_map/ppermute | solution.py:429
  26.3 0.0 copy-start.15
  26.4 0.1 pad_add_fusion.place
  26.4 0.0 copy-start.18
  26.4 0.0 copy-done.6
  26.4 0.0 copy-done.7
  26.4 0.0 copy-done.8
  26.4 0.0 copy-done.9
  26.5 0.0 copy-done.10
  26.5 0.6 copy-done.15
  27.0 0.1 copy-done.18
  27.1 0.0 copy-start
  27.1 1.2 copy-done
  28.3 0.0 copy-start.1
  28.3 0.9 copy-done.1
  29.3 0.0 copy-start.16
  29.3 0.7 copy-done.16
  29.9 0.0 copy-start.3
  30.0 0.0 copy-start.5
  30.0 0.0 copy-start.12
  30.0 0.0 copy-start.14
  30.0 0.9 prepare.1
  30.8 0.0 collective-permute-done.left
  30.8 0.0 collective-permute-done.1.right
  30.9 0.0 copy-start.19
  30.9 0.0 copy-done.3
  30.9 0.0 copy-done.5
  30.9 0.0 copy-done.12
  30.9 0.0 copy-done.14
  30.9 0.6 copy-done.19
  31.5 12.0 %before.1 = (f32[64,256]{1,0:T(8,128)S(1)}, f32[4,128]{1,0:T(4,128)S(1)}) custom-call(f32[184,128]{1,0:T(8,128)S(1)} %collective-permute-done.left, f32[64,256]{1,0:T(8,128)S(1)} %copy-done.5, f32[64,256]{1,0:T(8,128)S(1)} %copy-done.3, s32[1,256]{1,0:T(1,128)S(1)} %bitcast.8, s32[8,256]{1,0:T(8,128)S(1)} %copy-done.12, s32[8,256]{1,0:T(8,128)S(1)} %copy-done.14, ...), custom_call_target="tpu_custom_call" | custom-call | flops 2147483648 | bytes 1048576 | tf_op jit(solution)/shard_map/before/pallas_call | solution.py:410
  43.6 7.7 %all_to_all.15 = f32[8,4,128]{2,1,0:T(4,128)S(1)} all-to-all(f32[8,4,128]{2,1,0:T(4,128)S(1)} %broadcast_in_dim.12), channel_id=1, replica_groups=mesh['curve'=128,'group'=8] {'group'}, dimensions={0} | all-to-all | bytes 32768 | tf_op jit(solution)/shard_map/all_to_all | solution.py:438
  51.4 40.7 %all_to_all.16 = f32[32,4,128]{2,1,0:T(4,128)S(1)} all-to-all(f32[32,4,128]{2,1,0:T(4,128)S(1)} %broadcast_in_dim.13), channel_id=1, replica_groups={{0,8,16,24,32,40,48,56,64,72,80,88,96,104,112,120,128,136,144,152,160,1..., dimensions={0} | all-to-all | bytes 131072 | tf_op jit(solution)/shard_map/all_to_all | solution.py:438
  92.1 9.8 %all_to_all.17 = f32[4,32,4,128]{3,2,1,0:T(4,128)S(1)} all-to-all(f32[4,32,4,128]{3,2,1,0:T(4,128)S(1)} %broadcast_in_dim.14), channel_id=1, replica_groups={{0,256,512,768},{8,264,520,776},{16,272,528,784},{24,280,536,792},{32,2..., dimensions={0} | all-to-all | bytes 524288 | tf_op jit(solution)/shard_map/all_to_all | solution.py:438
  102.0 5.3 %coarse.1 = (f32[64,256]{1,0:T(8,128)S(1)}, f32[32,128]{1,0:T(8,128)S(1)}, f32[32,128]{1,0:T(8,128)S(1)}) custom-call(s32[2]{0:T(128)S(1)} %pad_add_fusion.place, f32[512,128]{1,0:T(8,128)S(1)} %bitcast.5, s32[24,128]{1,0:T(8,128)S(1)} %get-tuple-element.22.table, s32[8,1024]{1,0:T(8,128)S(1)} %copy-done.9, s32[8,1024]{1,0:T(8,128)S(1)} %copy-done.10, ...), custom_call_target="tpu_custom_call" | custom-call | flops 1073741824 | bytes 1048576 | tf_op jit(solution)/shard_map/coarse/pallas_call | solution.py:410
  107.3 1.9 %collective-permute-start.2 = (f32[32,128]{1,0:T(8,128)S(1)}, f32[32,128]{1,0:T(8,128)S(1)}, u32[]{:S(2)}, u32[]{:S(2)}) collective-permute-start(f32[32,128]{1,0:T(8,128)S(1)} %get-tuple-element.26), channel_id=1, source_target_pairs={{0,1},{1,2},{2,3},{3,4},{4,5},{5,6},{6,7},{7,8},{8,9},{9,10},{10,1... | collective-permute-start | bytes 49160 | tf_op jit(solution)/shard_map/ppermute | solution.py:429
  109.2 7.9 %collective-permute-start.3 = (f32[32,128]{1,0:T(8,128)S(1)}, f32[32,128]{1,0:T(8,128)S(1)}, u32[]{:S(2)}, u32[]{:S(2)}) collective-permute-start(f32[32,128]{1,0:T(8,128)S(1)} %get-tuple-element.28), channel_id=1, source_target_pairs={{1,0},{2,1},{3,2},{4,3},{5,4},{6,5},{7,6},{8,7},{9,8},{10,9},{11,1... | collective-permute-start | bytes 49160 | tf_op jit(solution)/shard_map/ppermute | solution.py:429
  117.1 0.0 collective-permute-done.2.left
  117.1 1.4 %collective-permute-done.3.right = f32[32,128]{1,0:T(8,128)S(1)} collective-permute-done((f32[32,128]{1,0:T(8,128)S(1)}, f32[32,128]{1,0:T(8,128)S(1)}, u32[]{:S(2)}, u32[]{:S(2)}) %collective-permute-start.3) | collective-permute-done | bytes 16416 | tf_op jit(solution)/shard_map/ppermute | solution.py:429
  118.5 3.1 %after.1 = f32[64,256]{1,0:T(8,128)} custom-call(f32[32,128]{1,0:T(8,128)S(1)} %collective-permute-done.2.left, f32[64,256]{1,0:T(8,128)S(1)} %get-tuple-element.27.field, f32[32,128]{1,0:T(8,128)S(1)} %collective-permute-done.3.right, f32[64,256]{1,0:T(8,128)S(1)} %copy-done.5, s32[1,256]{1,0:T(1,128)S(1)} %bitcast.9, s32[8,256]{1,0:T(8,128)S(1)} %copy-done.12, ...), custom_call_target="tpu_custom_call" | custom-call | flops 536870912 | bytes 1048576 | tf_op jit(solution)/shard_map/after/pallas_call | solution.py:410
  (4 shorter events, 0.1 us)
Async XLA Ops:
  0.0 0.7 copy-start.17
  0.7 0.8 copy-start.2
  1.5 0.8 copy-start.4
  2.4 0.7 copy-start.11
  3.1 0.7 copy-start.13
  3.8 22.7 %copy-start.6 = (f32[64,64]{1,0:T(8,128)S(1)}, f32[64,64]{1,0:T(8,128)}, u32[]{:S(2)}) copy-start(f32[64,64]{1,0:T(8,128)} %stiffness.1) | copy-start | bytes 49156
  3.8 22.7 %copy-start.7 = (f32[64,64]{1,0:T(8,128)S(1)}, f32[64,64]{1,0:T(8,128)}, u32[]{:S(2)}) copy-start(f32[64,64]{1,0:T(8,128)} %smoother.1) | copy-start | bytes 49156
  3.8 22.7 %copy-start.8 = (s32[2,4096]{1,0:T(2,128)S(1)}, s32[2,4096]{1,0:T(2,128)}, u32[]{:S(2)}) copy-start(s32[2,4096]{1,0:T(2,128)} %owners_three.1) | copy-start | bytes 98308
  3.8 22.7 %copy-start.9 = (s32[8,1024]{1,0:T(8,128)S(1)}, s32[8,1024]{1,0:T(8,128)}, u32[]{:S(2)}) copy-start(s32[8,1024]{1,0:T(8,128)} %coarse_neighbors.3) | copy-start | bytes 98308
  3.8 22.7 %copy-start.10 = (s32[8,1024]{1,0:T(8,128)S(1)}, s32[8,1024]{1,0:T(8,128)}, u32[]{:S(2)}) copy-start(s32[8,1024]{1,0:T(8,128)} %coarse_kinds.3) | copy-start | bytes 98308
  3.9 27.0 %collective-permute-start = (f32[184,128]{1,0:T(8,128)S(1)}, f32[184,128]{1,0:T(8,128)S(1)}, u32[]{:S(2)}, u32[]{:S(2)}) collective-permute-start(f32[184,128]{1,0:T(8,128)S(1)} %get-tuple-element.17), channel_id=1, source_target_pairs={{0,1},{1,2},{2,3},{3,4},{4,5},{5,6},{6,7},{7,8},{8,9},{9,10},{10,1... | collective-permute-start | bytes 282632 | tf_op jit(solution)/shard_map/ppermute | solution.py:429
  5.8 25.1 %collective-permute-start.1 = (f32[184,128]{1,0:T(8,128)S(1)}, f32[184,128]{1,0:T(8,128)S(1)}, u32[]{:S(2)}, u32[]{:S(2)}) collective-permute-start(f32[184,128]{1,0:T(8,128)S(1)} %get-tuple-element.18), channel_id=1, source_target_pairs={{1,0},{2,1},{3,2},{4,3},{5,4},{6,5},{7,6},{8,7},{9,8},{10,9},{11,1... | collective-permute-start | bytes 282632 | tf_op jit(solution)/shard_map/ppermute | solution.py:429
  26.3 0.7 copy-start.15
  26.4 0.7 copy-start.18
  27.1 1.2 copy-start
  28.3 0.9 copy-start.1
  29.3 0.7 copy-start.16
  29.9 0.9 copy-start.3
  30.0 0.9 copy-start.5
  30.0 0.9 copy-start.12
  30.0 0.9 copy-start.14
  30.9 0.7 copy-start.19
  107.3 9.8 %collective-permute-start.2 = (f32[32,128]{1,0:T(8,128)S(1)}, f32[32,128]{1,0:T(8,128)S(1)}, u32[]{:S(2)}, u32[]{:S(2)}) collective-permute-start(f32[32,128]{1,0:T(8,128)S(1)} %get-tuple-element.26), channel_id=1, source_target_pairs={{0,1},{1,2},{2,3},{3,4},{4,5},{5,6},{6,7},{7,8},{8,9},{9,10},{10,1... | collective-permute-start | bytes 49160 | tf_op jit(solution)/shard_map/ppermute | solution.py:429
  109.2 9.3 %collective-permute-start.3 = (f32[32,128]{1,0:T(8,128)S(1)}, f32[32,128]{1,0:T(8,128)S(1)}, u32[]{:S(2)}, u32[]{:S(2)}) collective-permute-start(f32[32,128]{1,0:T(8,128)S(1)} %get-tuple-element.28), channel_id=1, source_target_pairs={{1,0},{2,1},{3,2},{4,3},{5,4},{6,5},{7,6},{8,7},{9,8},{10,9},{11,1... | collective-permute-start | bytes 49160 | tf_op jit(solution)/shard_map/ppermute | solution.py:429
where the time goes:
time: 122 us
  blocking collectives  58.3 us (48%)
  starting transfers between devices  32.2 us (26%)
  Pallas kernels  21.5 us (18%)
  local copies, waits for them, and re-layouts  7.96 us (7%)
  waiting for transfers between devices  1.42 us (1%)
    all_to_all x3, blocking collectives, spread(): return lax.all_to_all(copies, axis, 0, 0, axis_index_groups=groups)  58.3 us
    ppermute x2, starting transfers between devices, both_ways(): lax.ppermute(down_part, AXES, down)  28.4 us
    pallas_call x5, Pallas kernels, call(): pl.pallas_call(kernel, out_shape=[jax.ShapeDtypeStruct(shape, dtype) for...  21.5 us
    unnamed x40, local copies, waits for them, and re-layouts  7.91 us
    ppermute x2, starting transfers between devices, both_ways(): lax.ppermute(up_part, AXES, up)  3.84 us
  transfers between devices with their start and end apart: 4, of which 1 were waited for; matrix products, arithmetic and copies ran while one was open for 0% of the time, Pallas kernels for 1%

commit v1 on v0

v1 whole, which is shorter than its diff:
```python
import jax
import jax.numpy as jnp
from jax import lax
from jax.experimental import pallas as pl
from jax.experimental.pallas import tpu as pltpu
from jax.sharding import PartitionSpec as P

HALO = 64
DAMPING = 0.7
F32 = jnp.float32
BF16 = jnp.bfloat16
VMEM_LIMIT = 40 * 1024 * 1024
PACK_LIMIT = 60 * 1024 * 1024


def halves(x):
    high = x.astype(BF16)
    return high, (x - high.astype(F32)).astype(BF16)


def nn(a, b):
    return lax.dot_general(a, b, (((1,), (0,)), ((), ())), preferred_element_type=F32)


def nt(a, b):
    return lax.dot_general(a, b, (((1,), (1,)), ((), ())), preferred_element_type=F32)


def corners(product):
    half = product.shape[1] // 2
    top, low = product[:64], product[64:]
    return top[:, :half] + (top[:, half:] + low[:, :half]) + low[:, half:]


def wide_dot(matrix_pair, x):
    high, low = halves(x)
    return corners(nn(matrix_pair, jnp.concatenate([high, low], axis=1)))


def stacked(x):
    return jnp.concatenate(halves(x), axis=0)


def folded(x):
    half = x.shape[0] // 2
    return x[:half] + x[half:]


def onehot_rows(row_count, columns):
    rows = lax.broadcasted_iota(jnp.int32, (row_count, columns.shape[1]), 0)
    return jnp.where(rows == columns, 1.0, 0.0).astype(BF16)


def left_by(x, lanes):
    size = x.shape[1]
    return pltpu.roll(x, (size - lanes) % size, axis=1)


def couple(values, kinds, own, coupling_pair):
    total = None
    for part in range(8):
        pieces = []
        for kind in range(4 * part, 4 * part + 4):
            if kind < 30:
                chosen = None
                for slot in range(8):
                    term = jnp.where(kinds[slot : slot + 1] == kind, values[slot], 0.0)
                    chosen = term if chosen is None else chosen + term
            elif kind == 30:
                chosen = own
            else:
                chosen = jnp.zeros_like(own)
            pieces.append(jnp.concatenate(halves(chosen), axis=1))
        block = jnp.concatenate(pieces, axis=0)
        product = nn(coupling_pair[:, 256 * part : 256 * part + 256], block)
        total = product if total is None else total + product
    return corners(total)


def fine_tile(window, offsets, kinds, coupling_pair):
    lanes = lax.broadcasted_iota(jnp.int32, offsets.shape, 1)
    targets = jnp.where(offsets != 0, lanes + offsets + HALO, -1)
    window_pair = stacked(window)
    values = []
    for slot in range(0, 8, 2):
        columns = jnp.concatenate([targets[slot : slot + 1], targets[slot + 1 : slot + 2]], axis=1)
        picked = folded(nn(window_pair, onehot_rows(256, columns)))
        values += [picked[:, :128], picked[:, 128:]]
    own = left_by(window, HALO)[:, :128]
    return couple(values, kinds, own, coupling_pair), own


def by_octant(x, octant):
    return jnp.concatenate([jnp.where(octant == which, x, 0.0) for which in range(8)], axis=0)


def restrict(x, slot, octant, restriction_pair, parents):
    mapped = wide_dot(restriction_pair, by_octant(x, octant))
    return folded(nt(stacked(mapped), onehot_rows(parents, slot)))


def prolong(x, slot, octant, back_pair):
    pulled = folded(nn(stacked(x), onehot_rows(x.shape[1], slot)))
    return wide_dot(back_pair, by_octant(pulled, octant))


def power(levels):
    return jnp.left_shift(jnp.ones_like(levels), levels).astype(F32)


def inverse_power(levels):
    return jnp.where(levels == 0, 1.0, jnp.where(levels == 1, 0.5, jnp.where(levels == 2, 0.25, 0.125)))


def own_lanes(ref, rows, block, per):
    share = 128 // per
    first = pl.multiple_of((block // share) * 128, 128)
    held = ref[rows, pl.ds(first, 128)]
    held = jnp.broadcast_to(held, (8, 128))
    if share > 1:
        held = pltpu.roll(held, lax.rem(128 - per * lax.rem(block, share), 128), axis=1)
    lanes = lax.broadcasted_iota(jnp.int32, (8, 128), 1)
    return jnp.where(lanes < per, held, -1)


def other_curve(member, group):
    return jnp.where(
        group == 0,
        jnp.maximum(member - 1, 0),
        jnp.where(group == 7, jnp.minimum(member + 1, 127), member),
    )


def prepare_kernel(
    place,
    couplings,
    stiffness,
    smoother,
    restriction,
    owners_one,
    owners_two,
    owners_three,
    coarse_neighbors,
    coarse_kinds,
    coarse_level,
    coupling_pair,
    smoother_pair,
    restriction_pair,
    back_pair,
    table,
):
    def store(target, first, x):
        high, low = halves(x)
        target[0:64, first : first + x.shape[1]] = high
        target[64:128, first : first + x.shape[1]] = low

    for part in range(15):
        store(
            coupling_pair,
            128 * part,
            jnp.concatenate([couplings[2 * part], couplings[2 * part + 1]], axis=1),
        )
    store(
        coupling_pair,
        1920,
        jnp.concatenate([stiffness[...], jnp.zeros((64, 64), F32)], axis=1),
    )
    store(smoother_pair, 0, DAMPING * smoother[...])
    for part in range(4):
        first, second = restriction[2 * part], restriction[2 * part + 1]
        store(restriction_pair, 128 * part, jnp.concatenate([first, second], axis=1))
        upright = jnp.concatenate([first, second], axis=0)
        square = jnp.concatenate([upright, jnp.zeros((128, 64), F32)], axis=1)
        store(back_pair, 128 * part, jnp.transpose(square)[0:64])

    member, group = place[0], place[1]
    other = other_curve(member, group)
    lanes = lax.broadcasted_iota(jnp.int32, (8, 128), 1)

    def row(at):
        return slice(at, at + 1)

    mine = own_lanes(owners_three, row(0), member, 32)
    theirs = own_lanes(owners_three, row(0), other, 32)
    theirs = jnp.where(theirs < 0, -1, theirs + 8)
    table[0:1] = jnp.concatenate([mine, theirs], axis=1)[0:1]
    table[1:2] = jnp.concatenate(
        [
            own_lanes(owners_three, row(1), member, 32),
            own_lanes(owners_three, row(1), other, 32),
        ],
        axis=1,
    )[0:1]
    level = jnp.maximum(own_lanes(coarse_level, row(0), member, 8), 0)
    zero = jnp.int32(0)
    for at, values in enumerate(
        (
            level,
            own_lanes(owners_one, row(0), group, 64),
            own_lanes(owners_one, row(1), group, 64),
            own_lanes(owners_two, row(0), zero, 128),
            own_lanes(owners_two, row(1), zero, 128),
            jnp.zeros_like(level),
        )
    ):
        table[2 + at : 3 + at] = jnp.concatenate([values, values], axis=1)[0:1]
    every = slice(0, 8)
    wanted, near_kinds = [], []
    for curve in (member, other):
        near = own_lanes(coarse_neighbors, every, curve, 8)
        near_kinds.append(jnp.where(near >= 0, own_lanes(coarse_kinds, every, curve, 8), -1))
        blocks = jnp.where((lanes >= 64) & (lanes < 72), 8 * curve + lanes - 64, -1)
        for slot in range(8):
            moved = pltpu.roll(near, 8 * slot, axis=1) if slot else near
            moved = jnp.broadcast_to(moved[slot : slot + 1], (8, 128))
            blocks = jnp.where((lanes >> 3) == slot, moved, blocks)
        wanted.append(blocks)
    wanted = jnp.concatenate(wanted, axis=1)[0:1]
    both_kinds = jnp.where(lanes < 8, near_kinds[0], pltpu.roll(near_kinds[1], 8, axis=1))
    shifted = coarse_neighbors[...] + 1
    facts = jnp.concatenate(
        [shifted >> 5, shifted & 31, coarse_kinds[...], jnp.zeros_like(shifted)], axis=0
    )
    facts = facts.astype(F32).astype(BF16)
    found = nn(facts, onehot_rows(1024, wanted)).astype(jnp.int32)
    table[8:16] = 32 * found[0:8] + found[8:16] - 1
    table[16:24] = found[16:24]
    table[24:32] = jnp.concatenate([both_kinds, both_kinds], axis=1)
    table[32:40] = jnp.broadcast_to(wanted, (8, 256))


def pack_kernel(
    place,
    right_side,
    start_field,
    block_level,
    neighbors,
    neighbor_kinds,
    owners_zero,
    owners_one,
    owners_two,
    up,
    down,
    field,
    facts,
    parents,
):
    lane = lax.broadcasted_iota(jnp.int32, (32, 128), 1)
    low, high = start_field[:, 0:128], start_field[:, 128:256]
    up[0:64] = high
    up[64:96] = jnp.where(lane < 64, left_by(low[0:32], 64), low[32:64])
    down[0:64] = low
    down[64:96] = jnp.where(lane < 64, high[0:32], left_by(high[32:64], 64))
    field[...] = start_field[...]
    facts[0:64] = right_side[...]
    facts[64:72] = neighbors[...].astype(F32)
    facts[72:80] = neighbor_kinds[...].astype(F32)
    facts[80:88] = jnp.broadcast_to(block_level[...], (8, 256)).astype(F32)
    parents[...] = jnp.concatenate([owners_zero[...]] * 4, axis=0)
    group = place[1]
    shared = [
        own_lanes(owners_one, slice(0, 1), group, 64),
        own_lanes(owners_one, slice(1, 2), group, 64),
        jnp.broadcast_to(owners_two[0:1, :], (8, 128)),
        jnp.broadcast_to(owners_two[1:2, :], (8, 128)),
    ]
    for target, columns in ((up, slice(128, 256)), (down, slice(0, 128))):
        target[96:184] = facts[:, columns]
        target[184:186] = owners_zero[:, columns].astype(F32)
        for at, values in enumerate(shared):
            target[186 + at : 187 + at] = values[0:1].astype(F32)
        target[190:192] = jnp.zeros((2, 128), F32)


def fine_step(window, here, coupling_pair):
    offsets = here[64:72].astype(jnp.int32)
    kinds = here[72:80].astype(jnp.int32)
    levels = here[80:81].astype(jnp.int32)
    applied, held = fine_tile(window, offsets, kinds, coupling_pair)
    return applied, held, here[0:64], levels


def before_kernel(
    left,
    start_field,
    facts,
    right,
    owners_zero,
    coupling_pair,
    smoother_pair,
    restriction_pair,
    table,
    iterate_out,
    part_out,
    first,
    second,
    facts_wide,
    facts_narrow,
    remainder,
):
    matrix = coupling_pair
    far_left, far_right = left[64:96], right[64:96]
    row = jnp.concatenate(
        [
            jnp.concatenate([left_by(far_left, 64), far_left], axis=0),
            left[0:64],
            start_field[...],
            right[0:64],
            jnp.concatenate([far_right, left_by(far_right, 64)], axis=0),
        ],
        axis=1,
    )
    first[...] = left_by(row, 64)[:, :640]
    wide = jnp.concatenate([left[96:184], facts[...], right[96:184]], axis=1)
    facts_wide[...] = wide
    facts_narrow[...] = left_by(wide, 64)[:, :384]

    def sweep(source, facts_of, target, tiles):
        for at in range(tiles):
            columns = slice(128 * at, 128 * at + 128)
            applied, held, rhs, levels = fine_step(
                source[:, 128 * at : 128 * at + 256], facts_of[:, columns], matrix[...]
            )
            change = wide_dot(smoother_pair[...], rhs * power(levels) - applied)
            target[:, columns] = held + change

    sweep(first, facts_wide, second, 4)
    sweep(second, facts_narrow, iterate_out, 3)
    for at in range(2):
        columns = slice(128 * at, 128 * at + 128)
        applied, held, rhs, levels = fine_step(
            iterate_out[:, 128 * at : 128 * at + 256], facts[:, columns], matrix[...]
        )
        remainder[:, columns] = rhs - inverse_power(levels) * applied

    r_pair = restriction_pair[...]
    one = restrict(remainder[...], owners_zero[0:1], owners_zero[1:2], r_pair, 128)
    two = restrict(one, table[3:4, :128], table[4:5, :128], r_pair, 128)
    three = restrict(two, table[5:6, :128], table[6:7, :128], r_pair, 128)
    four = restrict(three, table[0:1, :128], table[1:2, :128], r_pair, 128)
    four = four * power(table[2:3, :128])
    both = jnp.concatenate([four, left_by(four, 4)], axis=0)
    part_out[...] = jnp.transpose(both)[0:4]


def finish_kernel(
    place,
    gathered,
    table,
    left,
    right,
    owners_zero,
    coupling_pair,
    smoother_pair,
    back_pair,
    iterate,
    facts,
    out,
    window,
):
    group = place[1]
    field_pair = stacked(jnp.transpose(gathered[...]))
    s_pair = smoother_pair[...]
    matrix = coupling_pair[...]

    def gather(blocks):
        rows = jnp.where(blocks >= 0, 4 * (blocks >> 3) + (blocks & 3), -1)
        both = folded(nn(field_pair, onehot_rows(512, rows)))
        return jnp.where(((blocks >> 2) & 1) == 0, both[0:64], both[64:128])

    values = [wide_dot(s_pair, gather(table[8 + slot : 9 + slot])) for slot in range(8)]
    rhs = gather(table[32:33])
    once = wide_dot(s_pair, rhs)
    twice = []
    for half in (slice(0, 128), slice(128, 256)):
        applied = couple([v[:, half] for v in values], table[16:24, half], once[:, half], matrix)
        twice.append(once[:, half] + wide_dot(s_pair, rhs[:, half] - applied))
    twice = jnp.concatenate(twice, axis=1)

    lanes = lax.broadcasted_iota(jnp.int32, (64, 128), 1)

    def eights(x, first):
        mine = left_by(x, first)[:, :128] if first else x[:, :128]
        return jnp.where(lanes < 8, mine, left_by(x, 120 + first)[:, :128])

    held = eights(twice, 64)
    applied = couple([eights(twice, 8 * k) for k in range(8)], table[24:32, :128], held, matrix)
    correction = held + wide_dot(s_pair, eights(rhs, 64) - applied)

    b_pair = back_pair[...]
    from_left = left[184:192].astype(jnp.int32)
    from_right = right[184:192].astype(jnp.int32)
    theirs = jnp.where(group == 0, from_left, from_right)

    def shift(slots, by):
        return jnp.where(slots < 0, -1, slots + by)

    three = prolong(correction, table[0:1], table[1:2], b_pair)
    two = prolong(
        three,
        jnp.concatenate([table[5:6, :128], shift(theirs[4:5], 128)], axis=1),
        jnp.concatenate([table[6:7, :128], theirs[5:6]], axis=1),
        b_pair,
    )
    lane = lax.broadcasted_iota(jnp.int32, (8, 128), 1)
    left_slots = shift(from_left, jnp.where(group == 0, 128, 0))
    right_slots = shift(from_right, jnp.where(group == 7, 128, 0))
    mine = pltpu.roll(table[0:8, :128], 64, axis=1)
    one = prolong(
        two,
        jnp.concatenate(
            [jnp.where(lane < 64, left_slots[2:3], mine[3:4])[0:1], right_slots[2:3]], axis=1
        ),
        jnp.concatenate(
            [jnp.where(lane < 64, from_left[3:4], mine[4:5])[0:1], from_right[3:4]], axis=1
        ),
        b_pair,
    )
    zero = prolong(
        one,
        jnp.concatenate([from_left[0:1], owners_zero[0:1] + 64, from_right[0:1] + 128], axis=1),
        jnp.concatenate([from_left[1:2], owners_zero[1:2], from_right[1:2]], axis=1),
        b_pair,
    )
    window[...] = iterate[...] + left_by(zero, 64)[:, :384]

    for at in range(2):
        columns = slice(128 * at, 128 * at + 128)
        applied, held, rhs, levels = fine_step(
            window[:, 128 * at : 128 * at + 256], facts[:, columns], matrix
        )
        out[:, columns] = held + wide_dot(s_pair, rhs * power(levels) - applied)


def call(kernel, outs, scratch, name, flops, places, *args, limit=VMEM_LIMIT):
    spaces = {
        "s": pl.BlockSpec(memory_space=pltpu.SMEM),
        "v": pl.BlockSpec(memory_space=pltpu.VMEM),
        "h": pl.BlockSpec(memory_space=pltpu.HBM),
    }
    fetched = [at for at, place in enumerate(places) if place == "h"]

    def body(*refs):
        inputs = list(refs[: len(args)])
        rest = refs[len(args) :]
        if fetched:
            targets, arrived = rest[len(outs) : len(outs) + len(fetched)], rest[-1]
            rest = rest[: len(outs)] + rest[len(outs) + len(fetched) : -1]
            copies = [
                pltpu.make_async_copy(inputs[at], target, arrived.at[which])
                for which, (at, target) in enumerate(zip(fetched, targets))
            ]
            for copy in copies:
                copy.start()
            for copy in copies:
                copy.wait()
            for at, target in zip(fetched, targets):
                inputs[at] = target
        kernel(*inputs, *rest)

    shapes = [pltpu.VMEM(args[at].shape, args[at].dtype) for at in fetched]
    shapes += [pltpu.VMEM(shape, dtype) for shape, dtype in scratch]
    if fetched:
        shapes.append(pltpu.SemaphoreType.DMA((len(fetched),)))
    return pl.pallas_call(
        body,
        out_shape=[jax.ShapeDtypeStruct(shape, dtype) for shape, dtype in outs],
        in_specs=[spaces[place] for place in places],
        out_specs=[spaces["v"]] * len(outs),
        scratch_shapes=shapes,
        compiler_params=pltpu.CompilerParams(vmem_limit_bytes=limit),
        cost_estimate=pl.CostEstimate(flops=flops, bytes_accessed=1 << 20, transcendentals=0),
        name=name,
    )(*args)


AXES = ("curve", "group")


def both_ways(up_part, down_part):
    peers = lax.axis_size(AXES)
    up = [(i, i + 1) for i in range(peers - 1)]
    down = [(i + 1, i) for i in range(peers - 1)]
    return lax.ppermute(up_part, AXES, up), lax.ppermute(down_part, AXES, down)


DEPTH = 32
WIDTH = 4


def spread(x, axis, count, groups=None):
    copies = jnp.broadcast_to(x[None], (count,) + x.shape)
    return lax.all_to_all(copies, axis, 0, 0, axis_index_groups=groups)


def share_coarse(part):
    along_z = [[x * DEPTH + z for z in range(DEPTH)] for x in range(WIDTH)]
    along_x = [[x * DEPTH + z for x in range(WIDTH)] for z in range(DEPTH)]
    total = jnp.sum(spread(part, "group", 8), axis=0)
    column = spread(total, "curve", DEPTH, along_z)
    return spread(column, "curve", WIDTH, along_x)


def stage_pack(*args):
    outs = (
        ((192, 128), F32),
        ((192, 128), F32),
        ((64, 256), F32),
        ((88, 256), F32),
        ((8, 256), jnp.int32),
    )
    return call(pack_kernel, outs, (), "pack", 1 << 20, "shhhhhhhh", *args, limit=PACK_LIMIT)


def stage_prepare(*args):
    outs = (
        ((128, 2048), BF16),
        ((128, 64), BF16),
        ((128, 512), BF16),
        ((128, 512), BF16),
        ((40, 256), jnp.int32),
    )
    return call(prepare_kernel, outs, (), "prepare", 1 << 20, "svvvvvvvvvv", *args)


def stage_before(*args):
    outs = (((64, 384), F32), ((4, 128), F32))
    scratch = (
        ((64, 640), F32),
        ((64, 512), F32),
        ((88, 512), F32),
        ((88, 384), F32),
        ((64, 256), F32),
    )
    return call(before_kernel, outs, scratch, "before", 1 << 31, "v" * 9, *args)


def stage_finish(*args):
    outs = (((64, 256), F32),)
    return call(
        finish_kernel, outs, (((64, 384), F32),), "finish", 1 << 30, "s" + "v" * 10, *args
    )


def shards(
    right_side,
    start_field,
    block_level,
    neighbors,
    neighbor_kinds,
    owners_zero,
    owners_one,
    owners_two,
    owners_three,
    coarse_neighbors,
    coarse_kinds,
    coarse_level,
    stiffness,
    smoother,
    couplings,
    restriction,
):
    place = jnp.stack([lax.axis_index("curve"), lax.axis_index("group")]).astype(jnp.int32)
    up, down, field, facts, parents = stage_pack(
        place,
        right_side,
        start_field,
        block_level[None, :],
        neighbors,
        neighbor_kinds,
        owners_zero,
        owners_one,
        owners_two,
    )
    left, right = both_ways(up, down)
    coupling_pair, smoother_pair, restriction_pair, back_pair, table = stage_prepare(
        place,
        couplings,
        stiffness,
        smoother,
        restriction,
        owners_one,
        owners_two,
        owners_three,
        coarse_neighbors,
        coarse_kinds,
        coarse_level[None, :],
    )
    iterate, part = stage_before(
        left,
        field,
        facts,
        right,
        parents,
        coupling_pair,
        smoother_pair,
        restriction_pair,
        table,
    )
    gathered = share_coarse(part)
    gathered = gathered.reshape(-1, gathered.shape[-1])
    (out,) = stage_finish(
        place,
        gathered,
        table,
        left,
        right,
        parents,
        coupling_pair,
        smoother_pair,
        back_pair,
        iterate,
        facts,
    )
    return out


def solution(mesh):
    fine = P(None, ("curve", "group"))
    return jax.shard_map(
        shards,
        mesh=mesh,
        in_specs=(
            fine,
            fine,
            P(("curve", "group")),
            fine,
            fine,
            fine,
            P(None, "curve"),
            P(None, "curve"),
            P(),
            P(),
            P(),
            P(),
            P(),
            P(),
            P(),
            P(),
        ),
        out_specs=fine,
        check_vma=False,
    )
```

time: 122 us -> 111 us (0.910)
  starting transfers between devices: 32.2 us -> 22.5 us
  local copies, waits for them, and re-layouts: 7.96 us -> 4.21 us
  Pallas kernels: 21.5 us -> 24.5 us
  waiting for transfers between devices: 1.42 us -> 0.01 us
    ppermute x2 -> x1, starting transfers between devices: 28.4 us -> 20.5 us  [both_ways(): lax.ppermute(down_part, AXES, down)]
    unnamed x40 -> x30, local copies, waits for them, and re-layouts: 7.91 us -> 4.16 us
    pallas_call x5 -> x4, Pallas kernels: 21.5 us -> 24.5 us  [call(): pl.pallas_call(body, out_shape=[jax.ShapeDtypeStruct(shape, dtype) for sh...]
    ppermute x2 -> x1, starting transfers between devices: 3.84 us -> 1.92 us  [both_ways(): lax.ppermute(up_part, AXES, up)]
    ppermute x2 -> x1, waiting for transfers between devices: 1.41 us -> 0.01 us  [both_ways(): lax.ppermute(down_part, AXES, down)]
  transfers between devices with their start and end apart: 4 -> 2, of which waited for: 1 -> 0; matrix products, arithmetic and copies ran while one was open for 0% -> 0% of each run, Pallas kernels for 1% -> 1%
where the time goes in v1:
time: 111 us; the launch traced here: 110 us
  blocking collectives  58.3 us (53%)
  Pallas kernels  24.5 us (22%)
  starting transfers between devices  22.5 us (20%)
  local copies, waits for them, and re-layouts  4.21 us (4%)
    all_to_all x3, blocking collectives, spread(): return lax.all_to_all(copies, axis, 0, 0, axis_index_groups=groups)  58.3 us
    pallas_call x4, Pallas kernels, call(): pl.pallas_call(body, out_shape=[jax.ShapeDtypeStruct(shape, dtype) for sh...  24.5 us
    ppermute x1, starting transfers between devices, both_ways(): lax.ppermute(down_part, AXES, down)  20.5 us
    unnamed x30, local copies, waits for them, and re-layouts  4.16 us
  transfers between devices with their start and end apart: 2, of which 0 were waited for; matrix products, arithmetic and copies ran while one was open for 0% of the time, Pallas kernels for 1%

profile of v1, /device:TPU:2, one launch (start us, length us, event | category | flops | bytes accessed | tf_op | source)
XLA Modules:
  0.0 110.3 jit_solution(1509977038060954017)
XLA Ops:
  0.0 0.0 copy-start.8
  0.0 0.0 copy-start.7
  0.0 0.0 copy-start.9
  0.0 0.7 pad_add_fusion.refs_0_
  0.7 0.0 copy-start.6
  0.7 0.0 copy-start.2
  0.7 0.0 copy-start.3
  0.7 0.0 copy-start.4
  0.7 0.0 copy-start.5
  0.7 2.5 %pack.1 = (f32[192,128]{1,0:T(8,128)}, f32[192,128]{1,0:T(8,128)}, f32[64,256]{1,0:T(8,128)}, f32[88,256]{1,0:T(8,128)}, s32[8,256]{1,0:T(8,128)}) custom-call(s32[2]{0:T(128)} %pad_add_fusion.refs_0_, f32[64,256]{1,0:T(8,128)} %refs_1_.2, f32[64,256]{1,0:T(8,128)} %refs_2_.2, s32[1,256]{1,0:T(1,128)} %bitcast.7, s32[8,256]{1,0:T(8,128)} %refs_4_.2, ...), custom_call_target="tpu_custom_call" | custom-call | flops 1048576 | bytes 1048576 | tf_op jit(solution)/shard_map/pack/pallas_call | solution.py:465
  3.2 1.9 %collective-permute-start = (f32[192,128]{1,0:T(8,128)}, f32[192,128]{1,0:T(8,128)S(1)}, u32[]{:S(2)}, u32[]{:S(2)}) collective-permute-start(f32[192,128]{1,0:T(8,128)} %get-tuple-element.17), channel_id=1, source_target_pairs={{0,1},{1,2},{2,3},{3,4},{4,5},{5,6},{6,7},{7,8},{8,9},{9,10},{10,1... | collective-permute-start | bytes 294920 | tf_op jit(solution)/shard_map/ppermute | solution.py:484
  5.2 20.5 %collective-permute-start.1 = (f32[192,128]{1,0:T(8,128)}, f32[192,128]{1,0:T(8,128)S(1)}, u32[]{:S(2)}, u32[]{:S(2)}) collective-permute-start(f32[192,128]{1,0:T(8,128)} %get-tuple-element.20), channel_id=1, source_target_pairs={{1,0},{2,1},{3,2},{4,3},{5,4},{6,5},{7,6},{8,7},{9,8},{10,9},{11,1... | collective-permute-start | bytes 294920 | tf_op jit(solution)/shard_map/ppermute | solution.py:484
  25.7 0.0 copy-done.8
  25.7 0.0 copy-done.7
  25.7 0.0 copy-done.9
  25.7 0.0 copy-done.6
  25.7 0.0 copy-done.2
  25.8 0.0 copy-done.3
  25.8 0.0 copy-done.4
  25.8 0.0 copy-done.5
  25.8 0.0 copy-start
  25.8 1.2 %copy-done = f32[30,64,64]{2,1,0:T(8,128)S(1)} copy-done((f32[30,64,64]{2,1,0:T(8,128)S(1)}, f32[30,64,64]{2,1,0:T(8,128)}, u32[]{:S(2)}) %copy-start) | copy-done | bytes 491544
  27.0 0.0 copy-start.1
  27.0 0.9 copy-done.1
  27.9 0.0 copy-start.10
  27.9 0.7 copy-done.10
  28.6 0.0 copy-start.12
  28.6 0.0 copy-start.13
  28.6 1.0 prepare.1
  29.6 0.0 copy-start.14
  29.6 0.0 collective-permute-done.refs_0_.refs_3_
  29.6 0.0 collective-permute-done.1.refs_3_.refs_4_
  29.6 0.0 copy-done.12
  29.7 0.0 copy-done.13
  29.7 0.6 copy-done.14
  30.3 10.8 %before.1 = (f32[64,384]{1,0:T(8,128)S(1)}, f32[4,128]{1,0:T(4,128)S(1)}) custom-call(f32[192,128]{1,0:T(8,128)S(1)} %collective-permute-done.refs_0_.refs_3_, f32[64,256]{1,0:T(8,128)S(1)} %copy-done.13, f32[88,256]{1,0:T(8,128)S(1)} %copy-done.12, f32[192,128]{1,0:T(8,128)S(1)} %collective-permute-done.1.refs_3_.refs_4_, s32[8,256]{1,0:T(8,128)S(1)} %copy-done.14, ...), custom_call_target="tpu_custom_call" | custom-call | flops 2147483648 | bytes 1048576 | tf_op jit(solution)/shard_map/before/pallas_call | solution.py:465
  41.1 7.7 %all_to_all.15 = f32[8,4,128]{2,1,0:T(4,128)S(1)} all-to-all(f32[8,4,128]{2,1,0:T(4,128)S(1)} %broadcast_in_dim.12), channel_id=1, replica_groups=mesh['curve'=128,'group'=8] {'group'}, dimensions={0} | all-to-all | bytes 32768 | tf_op jit(solution)/shard_map/all_to_all | solution.py:493
  48.9 40.7 %all_to_all.16 = f32[32,4,128]{2,1,0:T(4,128)S(1)} all-to-all(f32[32,4,128]{2,1,0:T(4,128)S(1)} %broadcast_in_dim.13), channel_id=1, replica_groups={{0,8,16,24,32,40,48,56,64,72,80,88,96,104,112,120,128,136,144,152,160,1..., dimensions={0} | all-to-all | bytes 131072 | tf_op jit(solution)/shard_map/all_to_all | solution.py:493
  89.6 9.9 %all_to_all.17 = f32[4,32,4,128]{3,2,1,0:T(4,128)S(1)} all-to-all(f32[4,32,4,128]{3,2,1,0:T(4,128)S(1)} %broadcast_in_dim.28), channel_id=1, replica_groups={{0,256,512,768},{8,264,520,776},{16,272,528,784},{24,280,536,792},{32,2..., dimensions={0} | all-to-all | bytes 524288 | tf_op jit(solution)/shard_map/all_to_all | solution.py:493
  99.5 0.0 copy-start.11
  99.5 0.7 copy-done.11
  100.1 10.2 %finish.1 = f32[64,256]{1,0:T(8,128)} custom-call(s32[2]{0:T(128)S(1)} %copy-done.11, f32[512,128]{1,0:T(8,128)S(1)} %bitcast.5, s32[40,256]{1,0:T(8,128)S(1)} %get-tuple-element.25.refs_8_.refs_2_, f32[192,128]{1,0:T(8,128)S(1)} %collective-permute-done.refs_0_.refs_3_, f32[192,128]{1,0:T(8,128)S(1)} %collective-permute-done.1.refs_3_.refs_4_, ...), custom_call_target="tpu_custom_call" | custom-call | flops 1073741824 | bytes 1048576 | tf_op jit(solution)/shard_map/finish/pallas_call | solution.py:465
  (4 shorter events, 0.1 us)
Async XLA Ops:
  0.0 25.7 %copy-start.8 = (s32[1024]{0:T(1024)S(1)}, s32[1024]{0:T(1024)}, u32[]{:S(2)}) copy-start(s32[1024]{0:T(1024)} %param.27) | copy-start | bytes 12292
  0.0 25.7 %copy-start.7 = (s32[2,512]{1,0:T(2,128)S(1)}, s32[2,512]{1,0:T(2,128)}, u32[]{:S(2)}) copy-start(s32[2,512]{1,0:T(2,128)} %refs_5_.3) | copy-start | bytes 12292
  0.0 25.7 %copy-start.9 = (s32[2,128]{1,0:T(2,128)S(1)}, s32[2,128]{1,0:T(2,128)}, u32[]{:S(2)}) copy-start(s32[2,128]{1,0:T(2,128)} %refs_6_.3) | copy-start | bytes 3076
  0.7 25.1 %copy-start.6 = (s32[8,1024]{1,0:T(8,128)S(1)}, s32[8,1024]{1,0:T(8,128)}, u32[]{:S(2)}) copy-start(s32[8,1024]{1,0:T(8,128)} %refs_9_.1) | copy-start | bytes 98308
  0.7 25.1 %copy-start.2 = (f32[64,64]{1,0:T(8,128)S(1)}, f32[64,64]{1,0:T(8,128)}, u32[]{:S(2)}) copy-start(f32[64,64]{1,0:T(8,128)} %refs_2_.3) | copy-start | bytes 49156
  0.7 25.1 %copy-start.3 = (f32[64,64]{1,0:T(8,128)S(1)}, f32[64,64]{1,0:T(8,128)}, u32[]{:S(2)}) copy-start(f32[64,64]{1,0:T(8,128)} %refs_3_.1) | copy-start | bytes 49156
  0.7 25.1 %copy-start.4 = (s32[2,4096]{1,0:T(2,128)S(1)}, s32[2,4096]{1,0:T(2,128)}, u32[]{:S(2)}) copy-start(s32[2,4096]{1,0:T(2,128)} %refs_7_.3) | copy-start | bytes 98308
  0.7 25.1 %copy-start.5 = (s32[8,1024]{1,0:T(8,128)S(1)}, s32[8,1024]{1,0:T(8,128)}, u32[]{:S(2)}) copy-start(s32[8,1024]{1,0:T(8,128)} %refs_8_.3) | copy-start | bytes 98308
  3.2 26.4 %collective-permute-start = (f32[192,128]{1,0:T(8,128)}, f32[192,128]{1,0:T(8,128)S(1)}, u32[]{:S(2)}, u32[]{:S(2)}) collective-permute-start(f32[192,128]{1,0:T(8,128)} %get-tuple-element.17), channel_id=1, source_target_pairs={{0,1},{1,2},{2,3},{3,4},{4,5},{5,6},{6,7},{7,8},{8,9},{9,10},{10,1... | collective-permute-start | bytes 294920 | tf_op jit(solution)/shard_map/ppermute | solution.py:484
  5.2 24.5 %collective-permute-start.1 = (f32[192,128]{1,0:T(8,128)}, f32[192,128]{1,0:T(8,128)S(1)}, u32[]{:S(2)}, u32[]{:S(2)}) collective-permute-start(f32[192,128]{1,0:T(8,128)} %get-tuple-element.20), channel_id=1, source_target_pairs={{1,0},{2,1},{3,2},{4,3},{5,4},{6,5},{7,6},{8,7},{9,8},{10,9},{11,1... | collective-permute-start | bytes 294920 | tf_op jit(solution)/shard_map/ppermute | solution.py:484
  25.8 1.2 %copy-start = (f32[30,64,64]{2,1,0:T(8,128)S(1)}, f32[30,64,64]{2,1,0:T(8,128)}, u32[]{:S(2)}) copy-start(f32[30,64,64]{2,1,0:T(8,128)} %refs_1_.3) | copy-start | bytes 1474564
  27.0 0.9 copy-start.1
  27.9 0.7 copy-start.10
  28.6 1.0 copy-start.12
  28.6 1.0 copy-start.13
  29.6 0.7 copy-start.14
  99.5 0.7 copy-start.11

commit v2 on v1

--- a/solution.py
+++ b/solution.py
@@ -57,20 +57,35 @@
 
 
 def couple(values, kinds, own, coupling_pair):
+    values = [v.reshape(8, 8, 128) for v in values]
+    marks = [jnp.broadcast_to(kinds[slot : slot + 1], (8, 128)) for slot in range(8)]
+    for slot in range(8):
+        for later in range(slot + 1, 8):
+            same = marks[later] == marks[slot]
+            values[slot] = values[slot] + jnp.where(same[None], values[later], 0.0)
+            marks[later] = jnp.where(same, -1 - later, marks[later])
+    parts = []
+    for value in values:
+        high, low = halves(value.reshape(64, 128))
+        parts.append([half[16 * at : 16 * at + 16] for half in (high, low) for at in range(4)])
+    tags = [jnp.concatenate([mark, mark], axis=0).astype(jnp.int16) for mark in marks]
+    none = jnp.zeros((16, 128), BF16)
     total = None
     for part in range(8):
         pieces = []
         for kind in range(4 * part, 4 * part + 4):
             if kind < 30:
-                chosen = None
+                chosen = [none] * 8
                 for slot in range(8):
-                    term = jnp.where(kinds[slot : slot + 1] == kind, values[slot], 0.0)
-                    chosen = term if chosen is None else chosen + term
+                    hit = tags[slot] == jnp.asarray(kind, jnp.int16)
+                    chosen = [jnp.where(hit, new, old) for new, old in zip(parts[slot], chosen)]
+                high = jnp.concatenate(chosen[:4], axis=0)
+                low = jnp.concatenate(chosen[4:], axis=0)
             elif kind == 30:
-                chosen = own
+                high, low = halves(own)
             else:
-                chosen = jnp.zeros_like(own)
-            pieces.append(jnp.concatenate(halves(chosen), axis=1))
+                high = low = jnp.zeros((64, 128), BF16)
+            pieces.append(jnp.concatenate([high, low], axis=1))
         block = jnp.concatenate(pieces, axis=0)
         product = nn(coupling_pair[:, 256 * part : 256 * part + 256], block)
         total = product if total is None else total + product
@@ -112,6 +127,10 @@
     return jnp.where(levels == 0, 1.0, jnp.where(levels == 1, 0.5, jnp.where(levels == 2, 0.25, 0.125)))
 
 
+def position():
+    return lax.axis_index("curve"), lax.axis_index("group")
+
+
 def own_lanes(ref, rows, block, per):
     share = 128 // per
     first = pl.multiple_of((block // share) * 128, 128)
@@ -132,7 +151,6 @@
 
 
 def prepare_kernel(
-    place,
     couplings,
     stiffness,
     smoother,
@@ -173,7 +191,7 @@
         square = jnp.concatenate([upright, jnp.zeros((128, 64), F32)], axis=1)
         store(back_pair, 128 * part, jnp.transpose(square)[0:64])
 
-    member, group = place[0], place[1]
+    member, group = position()
     other = other_curve(member, group)
     lanes = lax.broadcasted_iota(jnp.int32, (8, 128), 1)
 
@@ -205,32 +223,32 @@
     ):
         table[2 + at : 3 + at] = jnp.concatenate([values, values], axis=1)[0:1]
     every = slice(0, 8)
-    wanted, near_kinds = [], []
-    for curve in (member, other):
-        near = own_lanes(coarse_neighbors, every, curve, 8)
-        near_kinds.append(jnp.where(near >= 0, own_lanes(coarse_kinds, every, curve, 8), -1))
-        blocks = jnp.where((lanes >= 64) & (lanes < 72), 8 * curve + lanes - 64, -1)
-        for slot in range(8):
-            moved = pltpu.roll(near, 8 * slot, axis=1) if slot else near
+    near = own_lanes(coarse_neighbors, every, member, 8)
+    near_kinds = jnp.where(near >= 0, own_lanes(coarse_kinds, every, member, 8), -1)
+    far = own_lanes(coarse_neighbors, every, other, 8)
+    far_kinds = jnp.where(far >= 0, own_lanes(coarse_kinds, every, other, 8), -1)
+    wanted = jnp.full((8, 128), -1, jnp.int32)
+    for slot in range(8):
+        for first, blocks in ((8 * slot, near), (64 + 8 * slot, far)):
+            moved = pltpu.roll(blocks, first, axis=1) if first else blocks
             moved = jnp.broadcast_to(moved[slot : slot + 1], (8, 128))
-            blocks = jnp.where((lanes >> 3) == slot, moved, blocks)
-        wanted.append(blocks)
-    wanted = jnp.concatenate(wanted, axis=1)[0:1]
-    both_kinds = jnp.where(lanes < 8, near_kinds[0], pltpu.roll(near_kinds[1], 8, axis=1))
+            wanted = jnp.where((lanes >= first) & (lanes < first + 8), moved, wanted)
+    sixteen = jnp.where(lanes < 8, 8 * member + lanes, 8 * other + lanes - 8)
+    sixteen = jnp.where(lanes < 16, sixteen, -1)
+    sixteen_kinds = jnp.where(lanes < 8, near_kinds, pltpu.roll(far_kinds, 8, axis=1))
     shifted = coarse_neighbors[...] + 1
     facts = jnp.concatenate(
         [shifted >> 5, shifted & 31, coarse_kinds[...], jnp.zeros_like(shifted)], axis=0
     )
     facts = facts.astype(F32).astype(BF16)
-    found = nn(facts, onehot_rows(1024, wanted)).astype(jnp.int32)
-    table[8:16] = 32 * found[0:8] + found[8:16] - 1
-    table[16:24] = found[16:24]
-    table[24:32] = jnp.concatenate([both_kinds, both_kinds], axis=1)
-    table[32:40] = jnp.broadcast_to(wanted, (8, 256))
+    found = nn(facts, onehot_rows(1024, wanted[0:1])).astype(jnp.int32)
+    links = 32 * found[0:8] + found[8:16] - 1
+    table[8:16] = jnp.concatenate([links, found[16:24]], axis=1)
+    table[16:24] = jnp.concatenate([sixteen_kinds, wanted], axis=1)
+    table[24:32] = jnp.concatenate([sixteen, sixteen], axis=1)
 
 
 def pack_kernel(
-    place,
     right_side,
     start_field,
     block_level,
@@ -257,7 +275,7 @@
     facts[72:80] = neighbor_kinds[...].astype(F32)
     facts[80:88] = jnp.broadcast_to(block_level[...], (8, 256)).astype(F32)
     parents[...] = jnp.concatenate([owners_zero[...]] * 4, axis=0)
-    group = place[1]
+    group = position()[1]
     shared = [
         own_lanes(owners_one, slice(0, 1), group, 64),
         own_lanes(owners_one, slice(1, 2), group, 64),
@@ -344,7 +362,6 @@
 
 
 def finish_kernel(
-    place,
     gathered,
     table,
     left,
@@ -358,7 +375,7 @@
     out,
     window,
 ):
-    group = place[1]
+    group = position()[1]
     field_pair = stacked(jnp.transpose(gathered[...]))
     s_pair = smoother_pair[...]
     matrix = coupling_pair[...]
@@ -368,24 +385,30 @@
         both = folded(nn(field_pair, onehot_rows(512, rows)))
         return jnp.where(((blocks >> 2) & 1) == 0, both[0:64], both[64:128])
 
-    values = [wide_dot(s_pair, gather(table[8 + slot : 9 + slot])) for slot in range(8)]
-    rhs = gather(table[32:33])
-    once = wide_dot(s_pair, rhs)
-    twice = []
-    for half in (slice(0, 128), slice(128, 256)):
-        applied = couple([v[:, half] for v in values], table[16:24, half], once[:, half], matrix)
-        twice.append(once[:, half] + wide_dot(s_pair, rhs[:, half] - applied))
-    twice = jnp.concatenate(twice, axis=1)
+    columns = [table[8 + slot : 9 + slot, :128] for slot in range(8)]
+    columns += [table[16:17, 128:], table[24:25, :128]]
+    values, known = [], []
+    for at in range(0, 10, 2):
+        both = gather(jnp.concatenate(columns[at : at + 2], axis=1))
+        swept = wide_dot(s_pair, both)
+        values += [swept[:, :128], swept[:, 128:]]
+        known += [both[:, :128], both[:, 128:]]
+    rhs, own_rhs = known[8:]
+    once, own_once = values[8:]
 
     lanes = lax.broadcasted_iota(jnp.int32, (64, 128), 1)
 
-    def eights(x, first):
-        mine = left_by(x, first)[:, :128] if first else x[:, :128]
-        return jnp.where(lanes < 8, mine, left_by(x, 120 + first)[:, :128])
-
-    held = eights(twice, 64)
-    applied = couple([eights(twice, 8 * k) for k in range(8)], table[24:32, :128], held, matrix)
-    correction = held + wide_dot(s_pair, eights(rhs, 64) - applied)
+    def eights(x, slot):
+        mine = left_by(x, 8 * slot) if slot else x
+        return jnp.where(lanes < 8, mine, left_by(x, 56 + 8 * slot))
+
+    kinds = table[16:24, :128]
+    applied = couple(values[:8], table[8:16, 128:], once, matrix)
+    twice = once + wide_dot(s_pair, rhs - applied)
+    applied = couple([eights(once, slot) for slot in range(8)], kinds, own_once, matrix)
+    own_twice = own_once + wide_dot(s_pair, own_rhs - applied)
+    applied = couple([eights(twice, slot) for slot in range(8)], kinds, own_twice, matrix)
+    correction = own_twice + wide_dot(s_pair, own_rhs - applied)
 
     b_pair = back_pair[...]
     from_left = left[184:192].astype(jnp.int32)
@@ -509,7 +532,7 @@
         ((88, 256), F32),
         ((8, 256), jnp.int32),
     )
-    return call(pack_kernel, outs, (), "pack", 1 << 20, "shhhhhhhh", *args, limit=PACK_LIMIT)
+    return call(pack_kernel, outs, (), "pack", 1 << 20, "hhhhhhhh", *args, limit=PACK_LIMIT)
 
 
 def stage_prepare(*args):
@@ -518,9 +541,9 @@
         ((128, 64), BF16),
         ((128, 512), BF16),
         ((128, 512), BF16),
-        ((40, 256), jnp.int32),
-    )
-    return call(prepare_kernel, outs, (), "prepare", 1 << 20, "svvvvvvvvvv", *args)
+        ((32, 256), jnp.int32),
+    )
+    return call(prepare_kernel, outs, (), "prepare", 1 << 20, "vvvvvvvvvv", *args)
 
 
 def stage_before(*args):
@@ -538,7 +561,7 @@
 def stage_finish(*args):
     outs = (((64, 256), F32),)
     return call(
-        finish_kernel, outs, (((64, 384), F32),), "finish", 1 << 30, "s" + "v" * 10, *args
+        finish_kernel, outs, (((64, 384), F32),), "finish", 1 << 30, "v" * 10, *args
     )
 
 
@@ -560,9 +583,7 @@
     couplings,
     restriction,
 ):
-    place = jnp.stack([lax.axis_index("curve"), lax.axis_index("group")]).astype(jnp.int32)
     up, down, field, facts, parents = stage_pack(
-        place,
         right_side,
         start_field,
         block_level[None, :],
@@ -574,7 +595,6 @@
     )
     left, right = both_ways(up, down)
     coupling_pair, smoother_pair, restriction_pair, back_pair, table = stage_prepare(
-        place,
         couplings,
         stiffness,
         smoother,
@@ -600,7 +620,6 @@
     gathered = share_coarse(part)
     gathered = gathered.reshape(-1, gathered.shape[-1])
     (out,) = stage_finish(
-        place,
         gathered,
         table,
         left,

time: 111 us -> 103 us (0.928)
  Pallas kernels: 24.5 us -> 18.3 us
    pallas_call x4, Pallas kernels: 24.5 us -> 18.3 us  [call(): pl.pallas_call(body, out_shape=[jax.ShapeDtypeStruct(shape, dtype) for sh...]
    unnamed x30 -> x26, local copies, waits for them, and re-layouts: 4.16 us -> 3.63 us
  transfers between devices with their start and end apart: 2 -> 2, of which waited for: 0 -> 0; matrix products, arithmetic and copies ran while one was open for 0% -> 0% of each run, Pallas kernels for 1% -> 0%
where the time goes in v2:
time: 103 us
  blocking collectives  58.3 us (57%)
  starting transfers between devices  22.5 us (22%)
  Pallas kernels  18.3 us (18%)
  local copies, waits for them, and re-layouts  3.68 us (4%)
    all_to_all x3, blocking collectives, spread(): return lax.all_to_all(copies, axis, 0, 0, axis_index_groups=groups)  58.3 us
    ppermute x1, starting transfers between devices, both_ways(): lax.ppermute(down_part, AXES, down)  20.5 us
    pallas_call x4, Pallas kernels, call(): pl.pallas_call(body, out_shape=[jax.ShapeDtypeStruct(shape, dtype) for sh...  18.3 us
    unnamed x26, local copies, waits for them, and re-layouts  3.63 us
  transfers between devices with their start and end apart: 2, of which 0 were waited for; matrix products, arithmetic and copies ran while one was open for 0% of the time, Pallas kernels for 0%

profile of v2, /device:TPU:2, one launch (start us, length us, event | category | flops | bytes accessed | tf_op | source)
XLA Modules:
  0.0 103.0 jit_solution(15224750842688950174)
XLA Ops:
  0.0 0.0 copy-start.2
  0.0 0.0 copy-start.3
  0.0 0.0 copy-start.4
  0.0 0.0 copy-start.5
  0.0 0.0 copy-start.8
  0.0 1.8 %pack.1 = (f32[192,128]{1,0:T(8,128)}, f32[192,128]{1,0:T(8,128)}, f32[64,256]{1,0:T(8,128)}, f32[88,256]{1,0:T(8,128)}, s32[8,256]{1,0:T(8,128)}) custom-call(f32[64,256]{1,0:T(8,128)} %refs_0_.2, f32[64,256]{1,0:T(8,128)} %refs_1_.2, s32[1,256]{1,0:T(1,128)} %bitcast.5, s32[8,256]{1,0:T(8,128)} %refs_3_.2, s32[8,256]{1,0:T(8,128)} %refs_4_.2, ...), custom_call_target="tpu_custom_call" | custom-call | flops 1048576 | bytes 1048576 | tf_op jit(solution)/shard_map/pack/pallas_call | solution.py:488
  1.8 0.0 copy-start.7
  1.8 1.9 %collective-permute-start = (f32[192,128]{1,0:T(8,128)}, f32[192,128]{1,0:T(8,128)S(1)}, u32[]{:S(2)}, u32[]{:S(2)}) collective-permute-start(f32[192,128]{1,0:T(8,128)} %get-tuple-element.17), channel_id=1, source_target_pairs={{0,1},{1,2},{2,3},{3,4},{4,5},{5,6},{6,7},{7,8},{8,9},{9,10},{10,1... | collective-permute-start | bytes 294920 | tf_op jit(solution)/shard_map/ppermute | solution.py:507
  3.8 0.0 copy-start.9
  3.8 20.5 %collective-permute-start.1 = (f32[192,128]{1,0:T(8,128)}, f32[192,128]{1,0:T(8,128)S(1)}, u32[]{:S(2)}, u32[]{:S(2)}) collective-permute-start(f32[192,128]{1,0:T(8,128)} %get-tuple-element.20), channel_id=1, source_target_pairs={{1,0},{2,1},{3,2},{4,3},{5,4},{6,5},{7,6},{8,7},{9,8},{10,9},{11,1... | collective-permute-start | bytes 294920 | tf_op jit(solution)/shard_map/ppermute | solution.py:507
  24.3 0.0 copy-done.2
  24.3 0.0 copy-done.3
  24.3 0.0 copy-done.4
  24.4 0.0 copy-done.5
  24.4 0.0 copy-done.8
  24.4 0.0 copy-done.7
  24.4 0.0 copy-done.9
  24.4 0.0 copy-start
  24.4 1.2 %copy-done = f32[30,64,64]{2,1,0:T(8,128)S(1)} copy-done((f32[30,64,64]{2,1,0:T(8,128)S(1)}, f32[30,64,64]{2,1,0:T(8,128)}, u32[]{:S(2)}) %copy-start) | copy-done | bytes 491544
  25.6 0.0 copy-start.1
  25.6 0.9 copy-done.1
  26.5 0.0 copy-start.6
  26.5 0.8 copy-done.6
  27.3 0.0 copy-start.10
  27.3 0.0 copy-start.11
  27.3 0.4 prepare.1
  27.8 0.0 copy-start.12
  27.8 0.0 collective-permute-done.refs_0_.refs_2_
  27.8 0.0 collective-permute-done.1.refs_3_
  27.8 0.4 copy-done.10
  28.2 0.0 copy-done.11
  28.2 0.3 copy-done.12
  28.5 8.6 %before.1 = (f32[64,384]{1,0:T(8,128)S(1)}, f32[4,128]{1,0:T(4,128)S(1)}) custom-call(f32[192,128]{1,0:T(8,128)S(1)} %collective-permute-done.refs_0_.refs_2_, f32[64,256]{1,0:T(8,128)S(1)} %copy-done.11, f32[88,256]{1,0:T(8,128)S(1)} %copy-done.10, f32[192,128]{1,0:T(8,128)S(1)} %collective-permute-done.1.refs_3_, s32[8,256]{1,0:T(8,128)S(1)} %copy-done.12, ...), custom_call_target="tpu_custom_call" | custom-call | flops 2147483648 | bytes 1048576 | tf_op jit(solution)/shard_map/before/pallas_call | solution.py:488
  37.0 7.7 %all_to_all.15 = f32[8,4,128]{2,1,0:T(4,128)S(1)} all-to-all(f32[8,4,128]{2,1,0:T(4,128)S(1)} %broadcast_in_dim.12), channel_id=1, replica_groups=mesh['curve'=128,'group'=8] {'group'}, dimensions={0} | all-to-all | bytes 32768 | tf_op jit(solution)/shard_map/all_to_all | solution.py:516
  44.8 40.7 %all_to_all.16 = f32[32,4,128]{2,1,0:T(4,128)S(1)} all-to-all(f32[32,4,128]{2,1,0:T(4,128)S(1)} %broadcast_in_dim.13), channel_id=1, replica_groups={{0,8,16,24,32,40,48,56,64,72,80,88,96,104,112,120,128,136,144,152,160,1..., dimensions={0} | all-to-all | bytes 131072 | tf_op jit(solution)/shard_map/all_to_all | solution.py:516
  85.6 9.8 %all_to_all.17 = f32[4,32,4,128]{3,2,1,0:T(4,128)S(1)} all-to-all(f32[4,32,4,128]{3,2,1,0:T(4,128)S(1)} %broadcast_in_dim.28), channel_id=1, replica_groups={{0,256,512,768},{8,264,520,776},{16,272,528,784},{24,280,536,792},{32,2..., dimensions={0} | all-to-all | bytes 524288 | tf_op jit(solution)/shard_map/all_to_all | solution.py:516
  95.4 7.5 %finish.1 = f32[64,256]{1,0:T(8,128)} custom-call(f32[512,128]{1,0:T(8,128)S(1)} %bitcast.3, s32[32,256]{1,0:T(8,128)S(1)} %get-tuple-element.25.refs_8_.refs_1_, f32[192,128]{1,0:T(8,128)S(1)} %collective-permute-done.refs_0_.refs_2_, f32[192,128]{1,0:T(8,128)S(1)} %collective-permute-done.1.refs_3_, s32[8,256]{1,0:T(8,128)S(1)} %copy-done.12, ...), custom_call_target="tpu_custom_call" | custom-call | flops 1073741824 | bytes 1048576 | tf_op jit(solution)/shard_map/finish/pallas_call | solution.py:488
  (4 shorter events, 0.1 us)
Async XLA Ops:
  0.0 24.3 %copy-start.2 = (f32[64,64]{1,0:T(8,128)S(1)}, f32[64,64]{1,0:T(8,128)}, u32[]{:S(2)}) copy-start(f32[64,64]{1,0:T(8,128)} %refs_1_.3) | copy-start | bytes 49156
  0.0 24.3 %copy-start.3 = (f32[64,64]{1,0:T(8,128)S(1)}, f32[64,64]{1,0:T(8,128)}, u32[]{:S(2)}) copy-start(f32[64,64]{1,0:T(8,128)} %refs_2_.1) | copy-start | bytes 49156
  0.0 24.3 %copy-start.4 = (s32[2,4096]{1,0:T(2,128)S(1)}, s32[2,4096]{1,0:T(2,128)}, u32[]{:S(2)}) copy-start(s32[2,4096]{1,0:T(2,128)} %refs_6_.3) | copy-start | bytes 98308
  0.0 24.3 %copy-start.5 = (s32[8,1024]{1,0:T(8,128)S(1)}, s32[8,1024]{1,0:T(8,128)}, u32[]{:S(2)}) copy-start(s32[8,1024]{1,0:T(8,128)} %refs_7_.3) | copy-start | bytes 98308
  0.0 24.3 %copy-start.8 = (s32[1024]{0:T(1024)S(1)}, s32[1024]{0:T(1024)}, u32[]{:S(2)}) copy-start(s32[1024]{0:T(1024)} %param.27) | copy-start | bytes 12292
  1.8 22.6 %copy-start.7 = (s32[2,512]{1,0:T(2,128)S(1)}, s32[2,512]{1,0:T(2,128)}, u32[]{:S(2)}) copy-start(s32[2,512]{1,0:T(2,128)} %refs_4_.3) | copy-start | bytes 12292
  1.8 25.9 %collective-permute-start = (f32[192,128]{1,0:T(8,128)}, f32[192,128]{1,0:T(8,128)S(1)}, u32[]{:S(2)}, u32[]{:S(2)}) collective-permute-start(f32[192,128]{1,0:T(8,128)} %get-tuple-element.17), channel_id=1, source_target_pairs={{0,1},{1,2},{2,3},{3,4},{4,5},{5,6},{6,7},{7,8},{8,9},{9,10},{10,1... | collective-permute-start | bytes 294920 | tf_op jit(solution)/shard_map/ppermute | solution.py:507
  3.8 20.6 %copy-start.9 = (s32[2,128]{1,0:T(2,128)S(1)}, s32[2,128]{1,0:T(2,128)}, u32[]{:S(2)}) copy-start(s32[2,128]{1,0:T(2,128)} %refs_5_.3) | copy-start | bytes 3076
  3.8 24.0 %collective-permute-start.1 = (f32[192,128]{1,0:T(8,128)}, f32[192,128]{1,0:T(8,128)S(1)}, u32[]{:S(2)}, u32[]{:S(2)}) collective-permute-start(f32[192,128]{1,0:T(8,128)} %get-tuple-element.20), channel_id=1, source_target_pairs={{1,0},{2,1},{3,2},{4,3},{5,4},{6,5},{7,6},{8,7},{9,8},{10,9},{11,1... | collective-permute-start | bytes 294920 | tf_op jit(solution)/shard_map/ppermute | solution.py:507
  24.4 1.2 %copy-start = (f32[30,64,64]{2,1,0:T(8,128)S(1)}, f32[30,64,64]{2,1,0:T(8,128)}, u32[]{:S(2)}) copy-start(f32[30,64,64]{2,1,0:T(8,128)} %refs_0_.3) | copy-start | bytes 1474564
  25.6 0.9 copy-start.1
  26.5 0.8 copy-start.6
  27.3 0.9 copy-start.10
  27.3 0.9 copy-start.11
  27.8 0.7 copy-start.12

commit v3 on v2

--- a/solution.py
+++ b/solution.py
@@ -92,7 +92,7 @@
     return corners(total)
 
 
-def fine_tile(window, offsets, kinds, coupling_pair):
+def look_up(window, offsets):
     lanes = lax.broadcasted_iota(jnp.int32, offsets.shape, 1)
     targets = jnp.where(offsets != 0, lanes + offsets + HALO, -1)
     window_pair = stacked(window)
@@ -101,8 +101,7 @@
         columns = jnp.concatenate([targets[slot : slot + 1], targets[slot + 1 : slot + 2]], axis=1)
         picked = folded(nn(window_pair, onehot_rows(256, columns)))
         values += [picked[:, :128], picked[:, 128:]]
-    own = left_by(window, HALO)[:, :128]
-    return couple(values, kinds, own, coupling_pair), own
+    return values, left_by(window, HALO)[:, :128]
 
 
 def by_octant(x, octant):
@@ -290,12 +289,23 @@
         target[190:192] = jnp.zeros((2, 128), F32)
 
 
-def fine_step(window, here, coupling_pair):
-    offsets = here[64:72].astype(jnp.int32)
-    kinds = here[72:80].astype(jnp.int32)
-    levels = here[80:81].astype(jnp.int32)
-    applied, held = fine_tile(window, offsets, kinds, coupling_pair)
-    return applied, held, here[0:64], levels
+def fine_image(source, facts, tiles, coupling_pair):
+    found = []
+    applied = []
+    for at in range(tiles):
+        here = facts[64:72, 128 * at : 128 * at + 128].astype(jnp.int32)
+        found.append(look_up(source[:, 128 * at : 128 * at + 256], here))
+        values, own = found[-1]
+        kinds = facts[72:80, 128 * at : 128 * at + 128].astype(jnp.int32)
+        applied.append(couple(values, kinds, own, coupling_pair))
+    held = jnp.concatenate([own for _, own in found], axis=1)
+    columns = slice(0, 128 * tiles)
+    return (
+        jnp.concatenate(applied, axis=1),
+        held,
+        facts[0:64, columns],
+        facts[80:81, columns].astype(jnp.int32),
+    )
 
 
 def before_kernel(
@@ -334,22 +344,14 @@
     facts_narrow[...] = left_by(wide, 64)[:, :384]
 
     def sweep(source, facts_of, target, tiles):
-        for at in range(tiles):
-            columns = slice(128 * at, 128 * at + 128)
-            applied, held, rhs, levels = fine_step(
-                source[:, 128 * at : 128 * at + 256], facts_of[:, columns], matrix[...]
-            )
-            change = wide_dot(smoother_pair[...], rhs * power(levels) - applied)
-            target[:, columns] = held + change
+        applied, held, rhs, levels = fine_image(source, facts_of, tiles, matrix)
+        change = wide_dot(smoother_pair[...], rhs * power(levels) - applied)
+        target[...] = held + change
 
     sweep(first, facts_wide, second, 4)
     sweep(second, facts_narrow, iterate_out, 3)
-    for at in range(2):
-        columns = slice(128 * at, 128 * at + 128)
-        applied, held, rhs, levels = fine_step(
-            iterate_out[:, 128 * at : 128 * at + 256], facts[:, columns], matrix[...]
-        )
-        remainder[:, columns] = rhs - inverse_power(levels) * applied
+    applied, held, rhs, levels = fine_image(iterate_out, facts, 2, matrix)
+    remainder[...] = rhs - inverse_power(levels) * applied
 
     r_pair = restriction_pair[...]
     one = restrict(remainder[...], owners_zero[0:1], owners_zero[1:2], r_pair, 128)
@@ -439,20 +441,19 @@
         ),
         b_pair,
     )
+    ends_slots = jnp.where(lane < 64, from_right + 128, from_left)[0:1]
+    ends_octants = jnp.where(lane < 64, from_right, from_left)[1:2]
     zero = prolong(
         one,
-        jnp.concatenate([from_left[0:1], owners_zero[0:1] + 64, from_right[0:1] + 128], axis=1),
-        jnp.concatenate([from_left[1:2], owners_zero[1:2], from_right[1:2]], axis=1),
+        jnp.concatenate([ends_slots, owners_zero[0:1] + 64], axis=1),
+        jnp.concatenate([ends_octants, owners_zero[1:2]], axis=1),
         b_pair,
     )
+    zero = jnp.concatenate([zero, zero[:, :128]], axis=1)
     window[...] = iterate[...] + left_by(zero, 64)[:, :384]
 
-    for at in range(2):
-        columns = slice(128 * at, 128 * at + 128)
-        applied, held, rhs, levels = fine_step(
-            window[:, 128 * at : 128 * at + 256], facts[:, columns], matrix
-        )
-        out[:, columns] = held + wide_dot(s_pair, rhs * power(levels) - applied)
+    applied, held, rhs, levels = fine_image(window, facts, 2, matrix)
+    out[...] = held + wide_dot(s_pair, rhs * power(levels) - applied)
 
 
 def call(kernel, outs, scratch, name, flops, places, *args, limit=VMEM_LIMIT):

time: 103 us -> 102 us (level)
  Pallas kernels: 18.3 us -> 17.1 us
    pallas_call x4, Pallas kernels: 18.3 us -> 17.1 us  [call(): pl.pallas_call(body, out_shape=[jax.ShapeDtypeStruct(shape, dtype) for sh...]
where the time goes in v3:
time: 102 us
  blocking collectives  58.3 us (57%)
  starting transfers between devices  22.5 us (22%)
  Pallas kernels  17.1 us (17%)
  local copies, waits for them, and re-layouts  3.68 us (4%)
    all_to_all x3, blocking collectives, spread(): return lax.all_to_all(copies, axis, 0, 0, axis_index_groups=groups)  58.3 us
    ppermute x1, starting transfers between devices, both_ways(): lax.ppermute(down_part, AXES, down)  20.5 us
    pallas_call x4, Pallas kernels, call(): pl.pallas_call(body, out_shape=[jax.ShapeDtypeStruct(shape, dtype) for sh...  17.1 us
    unnamed x26, local copies, waits for them, and re-layouts  3.63 us
  transfers between devices with their start and end apart: 2, of which 0 were waited for; matrix products, arithmetic and copies ran while one was open for 0% of the time, Pallas kernels for 0%

profile of v3, /device:TPU:2, one launch (start us, length us, event | category | flops | bytes accessed | tf_op | source)
XLA Modules:
  0.0 101.7 jit_solution(14517112886170977081)
XLA Ops:
  0.0 0.0 copy-start.2
  0.0 0.0 copy-start.3
  0.0 0.0 copy-start.4
  0.0 0.0 copy-start.5
  0.0 0.0 copy-start.8
  0.0 1.8 %pack.1 = (f32[192,128]{1,0:T(8,128)}, f32[192,128]{1,0:T(8,128)}, f32[64,256]{1,0:T(8,128)}, f32[88,256]{1,0:T(8,128)}, s32[8,256]{1,0:T(8,128)}) custom-call(f32[64,256]{1,0:T(8,128)} %refs_0_.2, f32[64,256]{1,0:T(8,128)} %refs_1_.2, s32[1,256]{1,0:T(1,128)} %bitcast.5, s32[8,256]{1,0:T(8,128)} %refs_3_.2, s32[8,256]{1,0:T(8,128)} %refs_4_.2, ...), custom_call_target="tpu_custom_call" | custom-call | flops 1048576 | bytes 1048576 | tf_op jit(solution)/shard_map/pack/pallas_call | solution.py:489
  1.8 0.0 copy-start.7
  1.8 1.9 %collective-permute-start = (f32[192,128]{1,0:T(8,128)}, f32[192,128]{1,0:T(8,128)S(1)}, u32[]{:S(2)}, u32[]{:S(2)}) collective-permute-start(f32[192,128]{1,0:T(8,128)} %get-tuple-element.17), channel_id=1, source_target_pairs={{0,1},{1,2},{2,3},{3,4},{4,5},{5,6},{6,7},{7,8},{8,9},{9,10},{10,1... | collective-permute-start | bytes 294920 | tf_op jit(solution)/shard_map/ppermute | solution.py:508
  3.8 0.0 copy-start.9
  3.8 20.5 %collective-permute-start.1 = (f32[192,128]{1,0:T(8,128)}, f32[192,128]{1,0:T(8,128)S(1)}, u32[]{:S(2)}, u32[]{:S(2)}) collective-permute-start(f32[192,128]{1,0:T(8,128)} %get-tuple-element.20), channel_id=1, source_target_pairs={{1,0},{2,1},{3,2},{4,3},{5,4},{6,5},{7,6},{8,7},{9,8},{10,9},{11,1... | collective-permute-start | bytes 294920 | tf_op jit(solution)/shard_map/ppermute | solution.py:508
  24.3 0.0 copy-done.2
  24.3 0.0 copy-done.3
  24.3 0.0 copy-done.4
  24.4 0.0 copy-done.5
  24.4 0.0 copy-done.8
  24.4 0.0 copy-done.7
  24.4 0.0 copy-done.9
  24.4 0.0 copy-start
  24.4 1.2 %copy-done = f32[30,64,64]{2,1,0:T(8,128)S(1)} copy-done((f32[30,64,64]{2,1,0:T(8,128)S(1)}, f32[30,64,64]{2,1,0:T(8,128)}, u32[]{:S(2)}) %copy-start) | copy-done | bytes 491544
  25.6 0.0 copy-start.1
  25.6 0.9 copy-done.1
  26.5 0.0 copy-start.6
  26.5 0.8 copy-done.6
  27.3 0.0 copy-start.10
  27.3 0.0 copy-start.11
  27.3 0.4 prepare.1
  27.8 0.0 copy-start.12
  27.8 0.0 collective-permute-done.refs_0_.refs_2_
  27.8 0.0 collective-permute-done.1.refs_3_
  27.8 0.4 copy-done.10
  28.2 0.0 copy-done.11
  28.2 0.3 copy-done.12
  28.5 7.6 %before.1 = (f32[64,384]{1,0:T(8,128)S(1)}, f32[4,128]{1,0:T(4,128)S(1)}) custom-call(f32[192,128]{1,0:T(8,128)S(1)} %collective-permute-done.refs_0_.refs_2_, f32[64,256]{1,0:T(8,128)S(1)} %copy-done.11, f32[88,256]{1,0:T(8,128)S(1)} %copy-done.10, f32[192,128]{1,0:T(8,128)S(1)} %collective-permute-done.1.refs_3_, s32[8,256]{1,0:T(8,128)S(1)} %copy-done.12, ...), custom_call_target="tpu_custom_call" | custom-call | flops 2147483648 | bytes 1048576 | tf_op jit(solution)/shard_map/before/pallas_call | solution.py:489
  36.1 7.7 %all_to_all.15 = f32[8,4,128]{2,1,0:T(4,128)S(1)} all-to-all(f32[8,4,128]{2,1,0:T(4,128)S(1)} %broadcast_in_dim.12), channel_id=1, replica_groups=mesh['curve'=128,'group'=8] {'group'}, dimensions={0} | all-to-all | bytes 32768 | tf_op jit(solution)/shard_map/all_to_all | solution.py:517
  43.9 40.7 %all_to_all.16 = f32[32,4,128]{2,1,0:T(4,128)S(1)} all-to-all(f32[32,4,128]{2,1,0:T(4,128)S(1)} %broadcast_in_dim.13), channel_id=1, replica_groups={{0,8,16,24,32,40,48,56,64,72,80,88,96,104,112,120,128,136,144,152,160,1..., dimensions={0} | all-to-all | bytes 131072 | tf_op jit(solution)/shard_map/all_to_all | solution.py:517
  84.6 9.8 %all_to_all.17 = f32[4,32,4,128]{3,2,1,0:T(4,128)S(1)} all-to-all(f32[4,32,4,128]{3,2,1,0:T(4,128)S(1)} %broadcast_in_dim.28), channel_id=1, replica_groups={{0,256,512,768},{8,264,520,776},{16,272,528,784},{24,280,536,792},{32,2..., dimensions={0} | all-to-all | bytes 524288 | tf_op jit(solution)/shard_map/all_to_all | solution.py:517
  94.5 7.3 %finish.1 = f32[64,256]{1,0:T(8,128)} custom-call(f32[512,128]{1,0:T(8,128)S(1)} %bitcast.3, s32[32,256]{1,0:T(8,128)S(1)} %get-tuple-element.25.refs_8_.refs_1_, f32[192,128]{1,0:T(8,128)S(1)} %collective-permute-done.refs_0_.refs_2_, f32[192,128]{1,0:T(8,128)S(1)} %collective-permute-done.1.refs_3_, s32[8,256]{1,0:T(8,128)S(1)} %copy-done.12, ...), custom_call_target="tpu_custom_call" | custom-call | flops 1073741824 | bytes 1048576 | tf_op jit(solution)/shard_map/finish/pallas_call | solution.py:489
  (4 shorter events, 0.1 us)
Async XLA Ops:
  0.0 24.3 %copy-start.2 = (f32[64,64]{1,0:T(8,128)S(1)}, f32[64,64]{1,0:T(8,128)}, u32[]{:S(2)}) copy-start(f32[64,64]{1,0:T(8,128)} %refs_1_.3) | copy-start | bytes 49156
  0.0 24.3 %copy-start.3 = (f32[64,64]{1,0:T(8,128)S(1)}, f32[64,64]{1,0:T(8,128)}, u32[]{:S(2)}) copy-start(f32[64,64]{1,0:T(8,128)} %refs_2_.1) | copy-start | bytes 49156
  0.0 24.3 %copy-start.4 = (s32[2,4096]{1,0:T(2,128)S(1)}, s32[2,4096]{1,0:T(2,128)}, u32[]{:S(2)}) copy-start(s32[2,4096]{1,0:T(2,128)} %refs_6_.3) | copy-start | bytes 98308
  0.0 24.3 %copy-start.5 = (s32[8,1024]{1,0:T(8,128)S(1)}, s32[8,1024]{1,0:T(8,128)}, u32[]{:S(2)}) copy-start(s32[8,1024]{1,0:T(8,128)} %refs_7_.3) | copy-start | bytes 98308
  0.0 24.3 %copy-start.8 = (s32[1024]{0:T(1024)S(1)}, s32[1024]{0:T(1024)}, u32[]{:S(2)}) copy-start(s32[1024]{0:T(1024)} %param.27) | copy-start | bytes 12292
  1.8 22.6 %copy-start.7 = (s32[2,512]{1,0:T(2,128)S(1)}, s32[2,512]{1,0:T(2,128)}, u32[]{:S(2)}) copy-start(s32[2,512]{1,0:T(2,128)} %refs_4_.3) | copy-start | bytes 12292
  1.8 25.9 %collective-permute-start = (f32[192,128]{1,0:T(8,128)}, f32[192,128]{1,0:T(8,128)S(1)}, u32[]{:S(2)}, u32[]{:S(2)}) collective-permute-start(f32[192,128]{1,0:T(8,128)} %get-tuple-element.17), channel_id=1, source_target_pairs={{0,1},{1,2},{2,3},{3,4},{4,5},{5,6},{6,7},{7,8},{8,9},{9,10},{10,1... | collective-permute-start | bytes 294920 | tf_op jit(solution)/shard_map/ppermute | solution.py:508
  3.8 20.6 %copy-start.9 = (s32[2,128]{1,0:T(2,128)S(1)}, s32[2,128]{1,0:T(2,128)}, u32[]{:S(2)}) copy-start(s32[2,128]{1,0:T(2,128)} %refs_5_.3) | copy-start | bytes 3076
  3.8 24.0 %collective-permute-start.1 = (f32[192,128]{1,0:T(8,128)}, f32[192,128]{1,0:T(8,128)S(1)}, u32[]{:S(2)}, u32[]{:S(2)}) collective-permute-start(f32[192,128]{1,0:T(8,128)} %get-tuple-element.20), channel_id=1, source_target_pairs={{1,0},{2,1},{3,2},{4,3},{5,4},{6,5},{7,6},{8,7},{9,8},{10,9},{11,1... | collective-permute-start | bytes 294920 | tf_op jit(solution)/shard_map/ppermute | solution.py:508
  24.4 1.2 %copy-start = (f32[30,64,64]{2,1,0:T(8,128)S(1)}, f32[30,64,64]{2,1,0:T(8,128)}, u32[]{:S(2)}) copy-start(f32[30,64,64]{2,1,0:T(8,128)} %refs_0_.3) | copy-start | bytes 1474564
  25.6 0.9 copy-start.1
  26.5 0.8 copy-start.6
  27.3 0.9 copy-start.10
  27.3 0.9 copy-start.11
  27.8 0.7 copy-start.12
